TPU v7x, 32 devices: a whole 2x2x4 slice. The times are simulated.
32 devices in a mesh: shard: 8 (over z, x), head: 4 (over y, core).
Axes of the slice: x: 2, y: 2, z: 4, core: 2. Of those that a mesh axis runs over, the one named last changes fastest.
Arguments:
- resid_in: float32 [2048, 1024], P(('shard', 'head')), may hold values from -6 to 6
- cotangent: float32 [2048, 1024], P(('shard', 'head')), may hold values from -6 to 6
- segment: int32 [2048], P('shard'), may hold values from 0 to 3, never falling along the last dimension, each value on 1 to 1024 neighbouring positions
- attn_gain: bfloat16 [1024], P('shard'), may hold values from 0.25 to 1.75
- w_query: bfloat16 [1024, 512], P('shard', 'head'), may hold values from -0.1875 to 0.1875
- w_key: bfloat16 [1024, 512], P('shard', 'head'), may hold values from -0.1875 to 0.1875
- w_value: bfloat16 [1024, 1024], P('shard', 'head'), may hold values from -0.1875 to 0.1875
- w_outgate: bfloat16 [1024, 1024], P('shard', 'head'), may hold values from -0.1875 to 0.1875
- w_low: bfloat16 [1024, 16], P('shard'), may hold values from -0.1875 to 0.1875
- w_rank: bfloat16 [16, 4, 128], P(None, 'head', 'shard'), may hold values from -1.5 to 1.5
- rank_bias: bfloat16 [4, 128], P('head', 'shard'), may hold values from -3 to 9
- head_gain: bfloat16 [256], P('shard'), may hold values from 0.25 to 1.75
- w_out: bfloat16 [1024, 1024], P('head', 'shard'), may hold values from -0.1875 to 0.1875
- mlp_gain: bfloat16 [1024], P('shard'), may hold values from 0.25 to 1.75
- w_gate: bfloat16 [1024, 2816], P('shard', 'head'), may hold values from -0.1875 to 0.1875
- w_up: bfloat16 [1024, 2816], P('shard', 'head'), may hold values from -0.1875 to 0.1875
- w_down: bfloat16 [2816, 1024], P('head', 'shard'), may hold values from -0.109375 to 0.109375
Outputs:
- resid_out: float32 [2048, 1024], P(('shard', 'head'))
- grad_in: float32 [2048, 1024], P(('shard', 'head'))
- grad_attn_gain: float32 [1024], P(('shard', 'head'))
- grad_w_query: float32 [1024, 512], P('shard', 'head')
- grad_w_key: float32 [1024, 512], P('shard', 'head')
- grad_w_value: float32 [1024, 1024], P('shard', 'head')
- grad_w_outgate: float32 [1024, 1024], P('shard', 'head')
- grad_w_low: float32 [1024, 16], P(('shard', 'head'))
- grad_w_rank: float32 [16, 4, 128], P(None, 'head', 'shard')
- grad_rank_bias: float32 [4, 128], P('head', 'shard')
- grad_head_gain: float32 [256], P(('shard', 'head'))
- grad_w_out: float32 [1024, 1024], P('head', 'shard')
- grad_mlp_gain: float32 [1024], P(('shard', 'head'))
- grad_w_gate: float32 [1024, 2816], P('shard', 'head')
- grad_w_up: float32 [1024, 2816], P('shard', 'head')
- grad_w_down: float32 [2816, 1024], P('head', 'shard')
Inputs may be any that keep to these rules, and one draw needn't show every extreme that they name: `segment`: document ids never fall along the token stream; each id covers 1 to 1024 consecutive tokens and some id covers exactly 1024.
All inputs are finite; a program needn't handle non-finite values.
Results may differ from a plain program's by a relative error of at most 0.019.
Values may be sent and summed in bfloat16 or wider, within the bound.
A program may use at most 128 MiB of HBM per device.

v0:
```python
import jax
import jax.numpy as jnp
from jax import lax
from jax.sharding import PartitionSpec as P

D = 1024
DK = 128
DV = 256
GATE_RANK = 16
GROUP = 64


EPS = 1e-06
HIGH_PRECISION = lax.Precision.HIGHEST


def entering(value, axis, join, neutral, backward):
    count = lax.axis_size(axis)
    place = lax.axis_index(axis)
    ahead = count - 1 - place if backward else place
    gathered = jax.tree.map(
        lambda a, kind: lax.all_gather(a.astype(kind), axis),
        value,
        jax.tree.map(lambda a: jnp.bfloat16 if a.dtype == jnp.float32 else a.dtype, value),
    )
    state = jax.tree.map(lambda a, e: jnp.zeros_like(a) + jnp.asarray(e, a.dtype), value, neutral)

    def one(turn, state):
        source = count - 1 - turn if backward else turn
        return join(
            state,
            jax.tree.map(
                lambda a, own: lax.dynamic_index_in_dim(a, source, 0, False).astype(own.dtype),
                gathered,
                value,
            ),
        )

    return lax.fori_loop(0, ahead, one, state)


def rms_scale(values):
    return lax.rsqrt(jnp.mean(values * values, axis=-1, keepdims=True) + EPS)


def group_pass(query, key, value_rows, logdec, segf, state, carry_seg):
    total = query.shape[0]
    heads = query.shape[1]
    count = total // GROUP
    scale = DK ** (-0.5)
    order = jnp.arange(GROUP)
    causal = order[:, None] >= order[None, :]

    def blocks(array):
        return array.reshape((count, GROUP) + array.shape[1:])

    def advance(carry, pieces):
        memory_state, prior = carry
        query_c, key_c, value_segment, decay_c, seg_c = pieces
        cumul = jnp.cumsum(decay_c, axis=0)
        query_decayed = query_c * jnp.exp(cumul) * scale
        key_inc = key_c * jnp.exp(-cumul)
        scores = jnp.einsum("thk,shk->hts", query_decayed, key_inc, precision=HIGH_PRECISION)
        joined = jnp.logical_and(causal, seg_c[:, None] == seg_c[None, :])
        scores = jnp.where(joined[None], scores, 0.0)
        inherit = (seg_c == prior).astype(jnp.float32)
        inside = jnp.einsum("hts,shv->thv", scores, value_segment, precision=HIGH_PRECISION)
        carried_state = jnp.einsum(
            "zsb,sbi->zsi", query_decayed, memory_state, precision=HIGH_PRECISION
        )
        result = inside + inherit[:, None, None] * carried_state
        final_result = cumul[-1]
        keep = (seg_c == seg_c[-1]).astype(jnp.float32)
        key_final_rows = key_c * jnp.exp(final_result[None] - cumul) * keep[:, None, None]
        linked_states = (seg_c[-1] == prior).astype(jnp.float32)
        memory_state = linked_states * jnp.exp(final_result)[
            :, :, None
        ] * memory_state + jnp.einsum(
            "zie,zir->ier", key_final_rows, value_segment, precision=HIGH_PRECISION
        )
        return ((memory_state, seg_c[-1]), result)

    (memory_state, last_seg), outs = lax.scan(
        advance,
        (state, carry_seg),
        (blocks(query), blocks(key), blocks(value_rows), blocks(logdec), blocks(segf)),
    )
    return (outs.reshape(total, heads, outs.shape[-1]), memory_state)


def combine(earlier, later):
    decay_e, state_e, first_e, last_e = earlier
    decay_l, state_l, first_l, last_l = later
    open_end = jnp.logical_or(last_e == 0.0, first_l == 0.0)
    link = jnp.where(open_end, 1.0, (last_e == first_l).astype(jnp.float32))
    pass_on = decay_l * link
    first_new = jnp.where(first_e == 0.0, first_l, first_e)
    last_new = jnp.where(last_l == 0.0, last_e, last_l)
    return (decay_e * pass_on, pass_on[:, :, None] * state_e + state_l, first_new, last_new)


def chain(element, backward):
    identity = (
        jnp.ones_like(element[0]),
        jnp.zeros_like(element[1]),
        jnp.zeros_like(element[2]),
        jnp.zeros_like(element[3]),
    )
    return entering(
        (element[0], element[1], element[2], element[3]), "shard", combine, identity, backward
    )


def on_device(
    resid_in,
    cotangent,
    segment,
    attn_gain,
    w_query,
    w_key,
    w_value,
    w_outgate,
    w_low,
    w_rank,
    rank_bias,
    head_gain,
    w_out,
    mlp_gain,
    w_gate,
    w_up,
    w_down,
):

    def fetch():
        return (
            lax.all_gather(attn_gain, "shard", axis=0, tiled=True),
            lax.all_gather(w_query, "shard", axis=0, tiled=True),
            lax.all_gather(w_key, "shard", axis=0, tiled=True),
            lax.all_gather(w_value, "shard", axis=0, tiled=True),
            lax.all_gather(w_outgate, "shard", axis=0, tiled=True),
            lax.all_gather(w_low, "shard", axis=0, tiled=True),
            lax.all_gather(w_rank, "shard", axis=2, tiled=True),
            lax.all_gather(rank_bias, "shard", axis=1, tiled=True),
            lax.all_gather(head_gain, "shard", axis=0, tiled=True),
            lax.all_gather(w_out, "shard", axis=1, tiled=True),
            lax.all_gather(mlp_gain, "shard", axis=0, tiled=True),
            lax.all_gather(w_gate, "shard", axis=0, tiled=True),
            lax.all_gather(w_up, "shard", axis=0, tiled=True),
            lax.all_gather(w_down, "shard", axis=1, tiled=True),
        )

    weights = fetch()
    gain_attn = weights[0].astype(jnp.float32)
    query_w, key_w, value_w, outgate_w, low_w, rank_w, bias_w = weights[1:8]
    gain_head = weights[8].astype(jnp.float32)
    out_w = weights[9]
    gain_mlp = weights[10].astype(jnp.float32)
    gate_w, up_w, down_w = weights[11:14]
    length = segment.shape[0]
    local_heads = query_w.shape[1] // DK
    scale = DK ** (-0.5)
    inv_attn = rms_scale(resid_in)
    normed_rows = (resid_in * inv_attn * gain_attn).astype(jnp.bfloat16)
    cot_rows = cotangent.astype(jnp.bfloat16)
    normed_in, cot_bf = (
        lax.all_gather(normed_rows, "head", axis=0, tiled=True),
        lax.all_gather(cot_rows, "head", axis=0, tiled=True),
    )
    query = jnp.dot(normed_in, query_w, preferred_element_type=jnp.float32).reshape(
        length, local_heads, DK
    )
    key = jnp.dot(normed_in, key_w, preferred_element_type=jnp.float32).reshape(
        length, local_heads, DK
    )
    value_rows = jnp.dot(normed_in, value_w, preferred_element_type=jnp.float32).reshape(
        length, local_heads, DV
    )
    outgate = jnp.dot(normed_in, outgate_w, preferred_element_type=jnp.float32).reshape(
        length, local_heads, DV
    )
    low = jnp.dot(normed_in, low_w, preferred_element_type=jnp.float32)
    rank_mat = rank_w.astype(jnp.float32).reshape(GATE_RANK, local_heads * DK)
    logit = jnp.dot(low, rank_mat, precision=HIGH_PRECISION) + bias_w.astype(jnp.float32).reshape(
        local_heads * DK
    )
    logdec = (jax.nn.log_sigmoid(logit) / 16.0).reshape(length, local_heads, DK)
    segf = segment.astype(jnp.float32) + 1.0
    first_seg = segf[:1]
    last_seg = segf[-1:]
    cumul = jnp.cumsum(logdec, axis=0)
    keep = (segf == last_seg[0]).astype(jnp.float32)
    key_final_rows = key * jnp.exp(cumul[-1][None] - cumul) * keep[:, None, None]
    summary_state = jnp.einsum("zie,zir->ier", key_final_rows, value_rows, precision=HIGH_PRECISION)
    through = jnp.exp(cumul[-1]) * (first_seg[0] == last_seg[0]).astype(jnp.float32)
    incoming = chain((through, summary_state, first_seg, last_seg), False)
    state_in = incoming[1]
    prior = incoming[3][0]

    def mixer(query_in, key_in, value_in, decay_in):
        return group_pass(query_in, key_in, value_in, decay_in, segf, state_in, prior)

    (mixed, state_out), mixer_back = jax.vjp(mixer, query, key, value_rows, logdec)
    inv_head = rms_scale(mixed)
    headnormed = mixed * inv_head * gain_head
    sigma_out = jax.nn.sigmoid(outgate)
    swish_out = outgate * sigma_out
    gated = (headnormed * swish_out).reshape(length, local_heads * DV).astype(jnp.bfloat16)
    resid_mid = resid_in + lax.psum_scatter(
        jnp.dot(gated, out_w, preferred_element_type=jnp.float32),
        "head",
        scatter_dimension=0,
        tiled=True,
    )
    inv_mlp = rms_scale(resid_mid)
    mid_rows = (resid_mid * inv_mlp * gain_mlp).astype(jnp.bfloat16)
    normed_mid = lax.all_gather(mid_rows, "head", axis=0, tiled=True)
    gate_pre = jnp.dot(normed_mid, gate_w, preferred_element_type=jnp.float32)
    up_pre = jnp.dot(normed_mid, up_w, preferred_element_type=jnp.float32)
    sigma_gate = jax.nn.sigmoid(gate_pre)
    active = gate_pre * sigma_gate
    hidden = (active * up_pre).astype(jnp.bfloat16)
    resid_out = resid_mid + lax.psum_scatter(
        jnp.dot(hidden, down_w, preferred_element_type=jnp.float32).astype(jnp.bfloat16),
        "head",
        scatter_dimension=0,
        tiled=True,
    ).astype(jnp.float32)
    weights = fetch()
    gain_attn = weights[0].astype(jnp.float32)
    query_w, key_w, value_w, outgate_w, low_w, rank_w = weights[1:7]
    gain_head = weights[8].astype(jnp.float32)
    out_w = weights[9]
    gain_mlp = weights[10].astype(jnp.float32)
    gate_w, up_w, down_w = weights[11:14]
    d_hidden = jnp.dot(cot_bf, down_w.T, preferred_element_type=jnp.float32)
    d_gatepre = (d_hidden * up_pre * sigma_gate * (1.0 + gate_pre * (1.0 - sigma_gate))).astype(
        jnp.bfloat16
    )
    d_uppre = (d_hidden * active).astype(jnp.bfloat16)
    grad_down = jnp.dot(hidden.T, cot_bf, preferred_element_type=jnp.float32)
    grad_gate = jnp.dot(normed_mid.T, d_gatepre, preferred_element_type=jnp.float32)
    grad_up = jnp.dot(normed_mid.T, d_uppre, preferred_element_type=jnp.float32)
    d_normmid = lax.psum_scatter(
        (
            jnp.dot(d_gatepre, gate_w.T, preferred_element_type=jnp.float32)
            + jnp.dot(d_uppre, up_w.T, preferred_element_type=jnp.float32)
        ).astype(jnp.bfloat16),
        "head",
        scatter_dimension=0,
        tiled=True,
    ).astype(jnp.float32)
    part_mlp_gain = jnp.sum(d_normmid * resid_mid * inv_mlp, axis=0)
    scaled_mid = gain_mlp * d_normmid
    d_mid = (
        cotangent
        + inv_mlp * scaled_mid
        - resid_mid * inv_mlp**3 * jnp.mean(scaled_mid * resid_mid, axis=-1, keepdims=True)
    )
    dmid_rows = d_mid.astype(jnp.bfloat16)
    dmid_bf = lax.all_gather(dmid_rows, "head", axis=0, tiled=True)
    d_gated = jnp.dot(dmid_bf, out_w.T, preferred_element_type=jnp.float32).reshape(
        length, local_heads, DV
    )
    grad_out = jnp.dot(gated.T, dmid_bf, preferred_element_type=jnp.float32)
    d_head = d_gated * swish_out
    d_outgate = (
        (d_gated * headnormed * sigma_out * (1.0 + outgate * (1.0 - sigma_out)))
        .reshape(length, local_heads * DV)
        .astype(jnp.bfloat16)
    )
    part_head_gain = jnp.sum(d_head * mixed * inv_head, axis=(0, 1))
    scaled_head = gain_head * d_head
    mixed_gradient = inv_head * scaled_head - mixed * inv_head**3 * jnp.mean(
        scaled_head * mixed, axis=-1, keepdims=True
    )
    inherit = (segf == prior).astype(jnp.float32)
    weighted_query = query * jnp.exp(cumul) * inherit[:, None, None] * scale
    local_gradient = jnp.einsum(
        "zie,zir->ier", weighted_query, mixed_gradient, precision=HIGH_PRECISION
    )
    through_all = jnp.exp(cumul[-1]) * (last_seg[0] == prior).astype(jnp.float32)
    empty_ids = jnp.zeros((1,), jnp.float32)
    outgoing = chain((through_all, local_gradient, empty_ids, empty_ids), True)
    d_query, d_key, d_value, d_logdec = mixer_back((mixed_gradient, outgoing[1]))
    query_bf = d_query.reshape(length, local_heads * DK).astype(jnp.bfloat16)
    key_bf = d_key.reshape(length, local_heads * DK).astype(jnp.bfloat16)
    value_bf = d_value.reshape(length, local_heads * DV).astype(jnp.bfloat16)
    d_logit = d_logdec.reshape(length, local_heads * DK) * jax.nn.sigmoid(-logit) / 16.0
    grad_bias = jnp.sum(d_logit, axis=0).reshape(local_heads, DK)
    grad_rank = jnp.dot(low.T, d_logit, precision=HIGH_PRECISION).reshape(
        GATE_RANK, local_heads, DK
    )
    d_low = (
        jnp.einsum(
            "thk,rhk->thr",
            d_logit.reshape(length, local_heads, DK),
            rank_w.astype(jnp.float32),
            precision=HIGH_PRECISION,
        )
        .astype(jnp.bfloat16)
        .reshape(length, local_heads * GATE_RANK)
    )
    part_low = (
        jnp.dot(normed_in.T, d_low, preferred_element_type=jnp.float32)
        .reshape(D, local_heads, GATE_RANK)
        .sum(axis=1)
    )
    grad_query = jnp.dot(normed_in.T, query_bf, preferred_element_type=jnp.float32)
    grad_key = jnp.dot(normed_in.T, key_bf, preferred_element_type=jnp.float32)
    grad_value = jnp.dot(normed_in.T, value_bf, preferred_element_type=jnp.float32)
    grad_outgate = jnp.dot(normed_in.T, d_outgate, preferred_element_type=jnp.float32)
    low_rows = jnp.tile(low_w.T, (local_heads, 1))
    total_term = jnp.dot(query_bf, query_w.T, preferred_element_type=jnp.float32)
    total_term = total_term + jnp.dot(key_bf, key_w.T, preferred_element_type=jnp.float32)
    total_term = total_term + jnp.dot(value_bf, value_w.T, preferred_element_type=jnp.float32)
    total_term = total_term + jnp.dot(d_outgate, outgate_w.T, preferred_element_type=jnp.float32)
    d_normin = lax.psum_scatter(
        (total_term + jnp.dot(d_low, low_rows, preferred_element_type=jnp.float32)).astype(
            jnp.bfloat16
        ),
        "head",
        scatter_dimension=0,
        tiled=True,
    ).astype(jnp.float32)
    part_attn_gain = jnp.sum(d_normin * resid_in * inv_attn, axis=0)
    scaled_in = gain_attn * d_normin
    grad_in = (
        d_mid
        + inv_attn * scaled_in
        - resid_in * inv_attn**3 * jnp.mean(scaled_in * resid_in, axis=-1, keepdims=True)
    )
    owned = (
        lax.psum_scatter(grad_query, "shard", scatter_dimension=0, tiled=True),
        lax.psum_scatter(grad_key, "shard", scatter_dimension=0, tiled=True),
        lax.psum_scatter(grad_value, "shard", scatter_dimension=0, tiled=True),
        lax.psum_scatter(grad_outgate, "shard", scatter_dimension=0, tiled=True),
        lax.psum_scatter(grad_rank, "shard", scatter_dimension=2, tiled=True),
        lax.psum_scatter(grad_bias, "shard", scatter_dimension=1, tiled=True),
        lax.psum_scatter(grad_out, "shard", scatter_dimension=1, tiled=True),
        lax.psum_scatter(grad_gate, "shard", scatter_dimension=0, tiled=True),
        lax.psum_scatter(grad_up, "shard", scatter_dimension=0, tiled=True),
        lax.psum_scatter(grad_down, "shard", scatter_dimension=1, tiled=True),
    )
    final_gate, final_up, final_down = (owned[7], owned[8], owned[9])
    small = (
        lax.psum_scatter(part_attn_gain, ("shard", "head"), scatter_dimension=0, tiled=True),
        lax.psum_scatter(part_low, ("shard", "head"), scatter_dimension=0, tiled=True),
        lax.psum_scatter(part_head_gain, ("shard", "head"), scatter_dimension=0, tiled=True),
        lax.psum_scatter(part_mlp_gain, ("shard", "head"), scatter_dimension=0, tiled=True),
    )
    return (
        resid_out,
        grad_in,
        small[0],
        owned[0],
        owned[1],
        owned[2],
        owned[3],
        small[1],
        owned[4],
        owned[5],
        small[2],
        owned[6],
        small[3],
        final_gate,
        final_up,
        final_down,
    )


def solution(mesh):
    in_specs = (
        P(("shard", "head"), None),
        P(("shard", "head"), None),
        P("shard"),
        P("shard"),
        P("shard", "head"),
        P("shard", "head"),
        P("shard", "head"),
        P("shard", "head"),
        P("shard", None),
        P(None, "head", "shard"),
        P("head", "shard"),
        P("shard"),
        P("head", "shard"),
        P("shard"),
        P("shard", "head"),
        P("shard", "head"),
        P("head", "shard"),
    )
    out_specs = (
        P(("shard", "head"), None),
        P(("shard", "head"), None),
        P(("shard", "head")),
        P("shard", "head"),
        P("shard", "head"),
        P("shard", "head"),
        P("shard", "head"),
        P(("shard", "head"), None),
        P(None, "head", "shard"),
        P("head", "shard"),
        P(("shard", "head")),
        P("head", "shard"),
        P(("shard", "head")),
        P("shard", "head"),
        P("shard", "head"),
        P("head", "shard"),
    )
    return jax.shard_map(
        on_device, mesh=mesh, in_specs=in_specs, out_specs=out_specs, check_vma=False
    )
```

profile of v0, /device:TPU:0, one launch (start us, length us, event | category | flops | bytes accessed | tf_op | source)
XLA Modules:
  0.0 1546.9 jit_solution(13096726731532107609)
XLA Ops:
  93.6 30.5 %all_gather.106 = bf16[16,1,128]{0,1,2:T(2,128)(2,1)S(1)} all-gather(bf16[16,1,16]{0,1,2:T(2,128)(2,1)S(1)} %copy.87), channel_id=1, replica_groups=mesh['shard'=8,'head'=4] {'shard'}, dimensions={2}, use_global_device_ids=true | all-gather | bytes 4608 | tf_op jit(solution)/shard_map/all_gather | solution.py:142
  144.6 31.4 %all_gather.112 = bf16[1024,256]{1,0:T(8,128)(2,1)S(1)} all-gather(bf16[128,256]{1,0:T(8,128)(2,1)S(1)} %copy-done.51), channel_id=1, replica_groups=mesh['shard'=8,'head'=4] {'shard'}, dimensions={0}, use_global_device_ids=true | all-gather | bytes 589824 | tf_op jit(solution)/shard_map/all_gather | solution.py:139
  176.4 30.8 %all_gather.111 = bf16[1024,128]{1,0:T(8,128)(2,1)S(1)} all-gather(bf16[128,128]{1,0:T(8,128)(2,1)S(1)} %copy-done.56), channel_id=1, replica_groups=mesh['shard'=8,'head'=4] {'shard'}, dimensions={0}, use_global_device_ids=true | all-gather | bytes 294912 | tf_op jit(solution)/shard_map/all_gather | solution.py:138
  207.9 31.2 %all-gather.1 = bf16[1024,256]{1,0:T(8,128)(2,1)S(1)} all-gather(bf16[128,256]{1,0:T(8,128)(2,1)S(1)} %convolution_convert_fusion.2), channel_id=3, replica_groups=mesh['shard'=8,'head'=4] {'shard'}, dimensions={0}, use_global_device_ids=true | all-gather | bytes 589824 | tf_op jit(solution)/shard_map/all_gather | solution.py:22
  239.9 51.1 %all_gather.117 = bf16[1024,128]{1,0:T(8,128)(2,1)S(1)} all-gather(bf16[128,128]{1,0:T(8,128)(2,1)S(1)} %copy-done.57), channel_id=1, replica_groups=mesh['shard'=8,'head'=4] {'shard'}, dimensions={0}, use_global_device_ids=true | all-gather | bytes 294912 | tf_op jit(solution)/shard_map/all_gather | solution.py:137
  291.7 34.4 %while.107 = (s32[]{:T(128)}, f32[1,128,256]{2,1,0:T(8,128)S(1)}, f32[]{:T(128)}, f32[4,64,1,256]{3,1,2,0:T(8,128)S(1)}, f32[4,64,1,128]{3,1,2,0:T(8,128)S(1)}, ...) while((s32[]{:T(128)}, f32[1,128,256]{2,1,0:T(8,128)S(1)}, ...), condition=%wide.region_7.8_spmd.clone.clone.clone, body=%wide.region_5.7_spmd.clone.clone.sunk.clone | while | flops 69980928 | bytes 1891127 | solution.py:83
  326.5 31.2 %all_gather.119 = bf16[1024,256]{1,0:T(8,128)(2,1)S(1)} all-gather(bf16[128,256]{1,0:T(8,128)(2,1)S(1)} %copy-done.52), channel_id=1, replica_groups=mesh['shard'=8,'head'=4] {'shard'}, dimensions={0}, use_global_device_ids=true | all-gather | bytes 589824 | tf_op jit(solution)/shard_map/all_gather | solution.py:140
  357.7 27.0 %all_gather.120 = bf16[256,1024]{1,0:T(8,128)(2,1)S(1)} all-gather(bf16[256,128]{1,0:T(8,128)(2,1)S(1)} %copy-done.53), channel_id=1, replica_groups=mesh['shard'=8,'head'=4] {'shard'}, dimensions={1}, use_global_device_ids=true | all-gather | bytes 589824 | tf_op jit(solution)/shard_map/all_gather | solution.py:145
  435.0 40.0 %all-gather.12.cloned.1.call-done = bf16[1024,704]{0,1:T(8,128)(2,1)} async-done(((bf16[128,704]{0,1:T(8,128)(2,1)}), bf16[1024,704]{0,1:T(8,128)(2,1)}) %all-gather.12.cloned.1.call-update) | async-done | bytes 1441808 | tf_op jit(solution)/shard_map/all_gather | solution.py:148
  477.8 40.0 %all-gather.14.cloned.1.call-done = bf16[704,1024]{1,0:T(8,128)(2,1)} async-done(((bf16[704,128]{1,0:T(8,128)(2,1)}), bf16[704,1024]{1,0:T(8,128)(2,1)}) %all-gather.14.cloned.1.call-update) | async-done | bytes 1441808 | tf_op jit(solution)/shard_map/all_gather | solution.py:149
  579.4 33.4 %all-gather.3 = bf16[1024,256]{1,0:T(8,128)(2,1)} all-gather(bf16[128,256]{1,0:T(8,128)(2,1)S(1)} %convolution_convert_fusion.1), channel_id=5, replica_groups=mesh['shard'=8,'head'=4] {'shard'}, dimensions={0}, use_global_device_ids=true | all-gather | bytes 589824 | tf_op jit(solution)/shard_map/all_gather | solution.py:22
  612.8 29.1 %while.105 = (s32[]{:T(128)}, f32[1,128,256]{2,1,0:T(8,128)S(1)}, f32[1]{0:T(128)}, s32[]{:T(128)}, bf16[8,1,128]{2,1,0:T(2,128)(2,1)}, /*index=5*/bf16[8,1]{0,1...) while((s32[]{:T(128)}, f32[1,128,256]{2,1,0:T(8,128)S(1)}, ...), condition=%wide.region_16.17_spmd.clone, body=%wide.region_15.16_spmd.sunk.clone | while | flops 98573 | bytes 329182 | solution.py:39
  642.1 49.0 %while.106 = (s32[]{:T(128)}, f32[1,128,256]{1,2,0:T(8,128)S(1)}, bf16[4,64,1,128]{3,1,2,0:T(8,128)(2,1)S(1)}, bf16[4,64,1,128]{3,1,2,0:T(8,128)(2,1)S(1)}, bf16...) while((s32[]{:T(128)}, f32[1,128,256]{1,2,0:T(8,128)S(1)}, ...), condition=%wide.region_21.22_spmd.clone, body=%wide.region_17.21_spmd.sunk.clone | while | flops 139268224 | bytes 3866513 | solution.py:83
  714.8 39.6 %reduce-scatter.50.cloned.1.call-done = f32[16,1]{1,0:T(8,128)} async-done(((f32[128,1]{1,0:T(8,128)}), f32[16,1]{1,0:T(8,128)}) %reduce-scatter.50.cloned.1.call-update) | async-done | bytes 80
  755.7 64.3 %reduce-scatter.48.cloned.1.call-done = f32[16,16]{1,0:T(8,128)} async-done(((f32[128,16]{1,0:T(8,128)}), f32[16,16]{1,0:T(8,128)}) %reduce-scatter.48.cloned.1.call-update) | async-done | bytes 1040
  821.3 135.7 %reduce-scatter.46.cloned.1.call-done = f32[32,16]{1,0:T(8,128)} async-done(((f32[1024,16]{1,0:T(8,128)}), f32[32,16]{1,0:T(8,128)}) %reduce-scatter.46.cloned.1.call-update) | async-done | bytes 2064
  978.0 39.7 %all-reduce.9 = (f32[1024]{0:T(1024)S(1)}, f32[256]{0:T(256)S(1)}, f32[1024]{0:T(1024)S(1)}) all-reduce(f32[1024]{0:T(1024)S(1)} %get-tuple-element.1270, f32[256]{0:T(256)S(1)} %copy-done.68, f32[1024]{0:T(1024)S(1)} %get-tuple-element.1268), channel_id=10, replica_groups=mesh['shard'=8,'head'=4] {'shard','head'}, use_global_device_ids=true, to_apply=%region_25.26.clone | all-reduce | flops 2304 | bytes 18432
  1043.3 65.5 %reduce-scatter.32.cloned.1.call-done = f32[128,128]{1,0:T(8,128)} async-done(((f32[1024,128]{1,0:T(8,128)}), f32[128,128]{1,0:T(8,128)}) %reduce-scatter.32.cloned.1.call-update) | async-done | bytes 65552 | tf_op jit(solution)/shard_map/reduce_scatter | solution.py:334
  1108.8 67.4 %reduce-scatter.34.cloned.1.call-done = f32[128,256]{1,0:T(8,128)} async-done(((f32[1024,256]{1,0:T(8,128)}), f32[128,256]{1,0:T(8,128)}) %reduce-scatter.34.cloned.1.call-update) | async-done | bytes 131088 | tf_op jit(solution)/shard_map/reduce_scatter | solution.py:335
  1176.2 67.3 %reduce-scatter.36.cloned.1.call-done = f32[128,256]{1,0:T(8,128)} async-done(((f32[1024,256]{1,0:T(8,128)}), f32[128,256]{1,0:T(8,128)}) %reduce-scatter.36.cloned.1.call-update) | async-done | bytes 131088 | tf_op jit(solution)/shard_map/reduce_scatter | solution.py:336
  1243.5 67.8 %reduce-scatter.38.cloned.1.call-done = f32[256,128]{1,0:T(8,128)} async-done(((f32[256,1024]{1,0:T(8,128)}), f32[256,128]{1,0:T(8,128)}) %reduce-scatter.38.cloned.1.call-update) | async-done | bytes 131088 | tf_op jit(solution)/shard_map/reduce_scatter | solution.py:339
  1311.3 75.7 %reduce-scatter.40.cloned.1.call-done = f32[128,704]{0,1:T(8,128)} async-done(((f32[1024,704]{0,1:T(8,128)}), f32[128,704]{0,1:T(8,128)}) %reduce-scatter.40.cloned.1.call-update) | async-done | bytes 360464 | tf_op jit(solution)/shard_map/reduce_scatter | solution.py:340
  1387.0 76.2 %reduce-scatter.42.cloned.1.call-done = f32[128,704]{0,1:T(8,128)} async-done(((f32[1024,704]{0,1:T(8,128)}), f32[128,704]{0,1:T(8,128)}) %reduce-scatter.42.cloned.1.call-update) | async-done | bytes 360464 | tf_op jit(solution)/shard_map/reduce_scatter | solution.py:341
  1463.3 76.3 %reduce-scatter.44.cloned.1.call-done = f32[704,128]{1,0:T(8,128)} async-done(((f32[704,1024]{1,0:T(8,128)}), f32[704,128]{1,0:T(8,128)}) %reduce-scatter.44.cloned.1.call-update) | async-done | bytes 360464 | tf_op jit(solution)/shard_map/reduce_scatter | solution.py:342
  (518 shorter events, 385.3 us)
Async XLA Ops:
  8.0 85.5 %copy-start.66 = (bf16[16,1,16]{2,0,1:T(8,128)(2,1)S(1)}, bf16[16,1,16]{2,0,1:T(8,128)(2,1)}, u32[]{:S(2)}) copy-start(bf16[16,1,16]{2,0,1:T(8,128)(2,1)} %param.34) | copy-start | bytes 1540
  8.0 407.9 %reduce-scatter.22.cloned.1.call-start = ((), (), s32[]{:S(2)}) async-start(), calls=%async_computation.15 | async-start | bytes 1310720 | tf_op jit(solution)/shard_map/reduce_scatter | solution.py:208
  59.9 84.7 %copy-start.51 = (bf16[128,256]{1,0:T(8,128)(2,1)S(1)}, bf16[128,256]{1,0:T(8,128)(2,1)}, u32[]{:S(2)}) copy-start(bf16[128,256]{1,0:T(8,128)(2,1)} %param.31) | copy-start | bytes 196612
  387.8 44.4 %all-gather.10.cloned.1.call-start = ((), (), s32[]{:S(2)}) async-start(), calls=%async_computation.16 | async-start | bytes 1622016 | tf_op jit(solution)/shard_map/all_gather | solution.py:147
  388.4 86.6 %all-gather.12.cloned.1.call-start = ((), (), s32[]{:S(2)}) async-start(), calls=%async_computation.17 | async-start | bytes 1622016 | tf_op jit(solution)/shard_map/all_gather | solution.py:148
  389.0 128.9 %all-gather.14.cloned.1.call-start = ((), (), s32[]{:S(2)}) async-start(), calls=%async_computation.18 | async-start | bytes 1622016 | tf_op jit(solution)/shard_map/all_gather | solution.py:149
  389.6 158.7 %reduce-scatter.26.cloned.1.call-start = ((), (), s32[]{:S(2)}) async-start(), calls=%async_computation.20 | async-start | bytes 655360 | tf_op jit(solution)/shard_map/reduce_scatter | solution.py:243
  524.3 44.1 %reduce-scatter.24.cloned.1.call-start = ((), (), s32[]{:S(2)}) async-start(), calls=%async_computation.19 | async-start | bytes 655360 | tf_op jit(solution)/shard_map/reduce_scatter | solution.py:222
  527.9 226.5 %reduce-scatter.50.cloned.1.call-start = ((), (), s32[]{:S(2)}) async-start(), calls=%async_computation.32 | async-start | bytes 73728
  694.9 125.0 %reduce-scatter.48.cloned.1.call-start = ((), (), s32[]{:S(2)}) async-start(), calls=%async_computation.31 | async-start | bytes 73728
  696.9 260.1 %reduce-scatter.46.cloned.1.call-start = ((), (), s32[]{:S(2)}) async-start(), calls=%async_computation.30 | async-start | bytes 540672
  698.2 278.6 %reduce-scatter.28.cloned.1.call-start = ((), (), s32[]{:S(2)}) async-start(), calls=%async_computation.21 | async-start | bytes 655360 | tf_op jit(solution)/shard_map/reduce_scatter | solution.py:317
  699.4 343.9 %reduce-scatter.30.cloned.1.call-start = ((), (), s32[]{:S(2)}) async-start(), calls=%async_computation.22 | async-start | bytes 589824 | tf_op jit(solution)/shard_map/reduce_scatter | solution.py:333
  700.6 408.1 %reduce-scatter.32.cloned.1.call-start = ((), (), s32[]{:S(2)}) async-start(), calls=%async_computation.23 | async-start | bytes 589824 | tf_op jit(solution)/shard_map/reduce_scatter | solution.py:334
  701.9 474.3 %reduce-scatter.34.cloned.1.call-start = ((), (), s32[]{:S(2)}) async-start(), calls=%async_computation.24 | async-start | bytes 1179648 | tf_op jit(solution)/shard_map/reduce_scatter | solution.py:335
  703.3 540.2 %reduce-scatter.36.cloned.1.call-start = ((), (), s32[]{:S(2)}) async-start(), calls=%async_computation.25 | async-start | bytes 1179648 | tf_op jit(solution)/shard_map/reduce_scatter | solution.py:336
  704.7 606.6 %reduce-scatter.38.cloned.1.call-start = ((), (), s32[]{:S(2)}) async-start(), calls=%async_computation.26 | async-start | bytes 1179648 | tf_op jit(solution)/shard_map/reduce_scatter | solution.py:339
  706.2 680.9 %reduce-scatter.40.cloned.1.call-start = ((), (), s32[]{:S(2)}) async-start(), calls=%async_computation.27 | async-start | bytes 3244032 | tf_op jit(solution)/shard_map/reduce_scatter | solution.py:340
  708.4 754.9 %reduce-scatter.42.cloned.1.call-start = ((), (), s32[]{:S(2)}) async-start(), calls=%async_computation.28 | async-start | bytes 3244032 | tf_op jit(solution)/shard_map/reduce_scatter | solution.py:341
  711.5 828.1 %reduce-scatter.44.cloned.1.call-start = ((), (), s32[]{:S(2)}) async-start(), calls=%async_computation.29 | async-start | bytes 3244032 | tf_op jit(solution)/shard_map/reduce_scatter | solution.py:342
  714.8 262.0 %copy-start.63 = (f32[64]{0:T(128)S(1)}, f32[64]{0:T(128)}, u32[]{:S(2)}) copy-start(f32[64]{0:T(128)} %copy-done.62) | copy-start | bytes 772
  714.8 263.1 %copy-start.68 = (f32[256]{0:T(256)S(1)}, f32[256]{0:T(256)}, u32[]{:S(2)}) copy-start(f32[256]{0:T(256)} %get-tuple-element.1266) | copy-start | bytes 3076
  714.8 304.6 %copy-start.32 = (f32[64,1024]{1,0:T(8,128)S(1)}, f32[64,1024]{1,0:T(8,128)}, u32[]{:S(2)}) copy-start(f32[64,1024]{1,0:T(8,128)} %get-tuple-element.1409) | copy-start | bytes 786436
  714.8 304.6 %copy-start.71 = (f32[64]{0:T(128)S(1)}, f32[64]{0:T(128)}, u32[]{:S(2)}) copy-start(f32[64]{0:T(128)} %get-tuple-element.1447) | copy-start | bytes 772
  (73 other events, 1743.9 us)
Sparse Core Ops, SparseCore 0:
  387.9 23.7 reduce-scatter.21
  524.5 19.8 reduce-scatter.25
  546.8 21.6 reduce-scatter.23
Sparse Core Ops, SparseCore 1:
  390.3 41.8 all-gather.9
  434.1 40.9 all-gather.11
  476.9 40.9 all-gather.13
  695.0 59.4 reduce-scatter.49
  758.4 61.5 reduce-scatter.47
  822.2 134.7 reduce-scatter.45
  959.4 17.4 reduce-scatter.27
  980.6 62.6 reduce-scatter.29
  1047.1 61.7 reduce-scatter.31
  1112.8 63.4 reduce-scatter.33
  1180.1 63.4 reduce-scatter.35
  1247.5 63.7 reduce-scatter.37
  1315.3 71.6 reduce-scatter.39
  1391.2 72.0 reduce-scatter.41
  1467.4 72.1 reduce-scatter.43
where the time goes:
time: 1550 us
  waiting for transfers between devices  884 us (57%)
  blocking collectives  455 us (29%)
  matrix products  60.1 us (4%)
  local copies, waits for them, and re-layouts  60 us (4%)
  other arithmetic  47.6 us (3%)
  loops' own time  19.8 us (1%)
  between operations  19.7 us (1%)
    unnamed x21, waiting for transfers between devices  241 us
    all_gather x4, blocking collectives, entering(): lax.all_gather(a.astype(kind), axis)  99.5 us
    reduce_scatter x1, waiting for transfers between devices, on_device(): lax.psum_scatter(grad_down, 'shard', scatter_dimension=1, tiled=True)  76.3 us
    reduce_scatter x1, waiting for transfers between devices, on_device(): lax.psum_scatter(grad_up, 'shard', scatter_dimension=0, tiled=True)  76.2 us
    reduce_scatter x1, waiting for transfers between devices, on_device(): lax.psum_scatter(grad_gate, 'shard', scatter_dimension=0, tiled=True)  75.7 us
    reduce_scatter x1, waiting for transfers between devices, on_device(): lax.psum_scatter(grad_out, 'shard', scatter_dimension=1, tiled=True)  67.8 us
    reduce_scatter x1, waiting for transfers between devices, on_device(): lax.psum_scatter(grad_value, 'shard', scatter_dimension=0, tiled=True)  67.4 us
    reduce_scatter x1, waiting for transfers between devices, on_device(): lax.psum_scatter(grad_outgate, 'shard', scatter_dimension=0, tiled=True)  67.3 us
  transfers between devices with their start and end apart: 18, of which 16 were waited for; matrix products, arithmetic and copies ran while one was open for 2% of the time, Pallas kernels for 0%

commit v1 on v0

v1 whole, which is shorter than its diff:
```python
import functools

import jax
import jax.numpy as jnp
from jax import lax
from jax.experimental import pallas as pl
from jax.experimental.pallas import tpu as pltpu
from jax.sharding import PartitionSpec as P

D = 1024
DK = 128
DV = 256
GATE_RANK = 16
GROUP = 64
LANE = 128
MESH = pl.DeviceIdType.MESH


EPS = 1e-06
HIGH_PRECISION = lax.Precision.HIGHEST


def ring_index(pos, n):
    return jnp.where(pos < n // 2, 2 * pos, 2 * (n - 1 - pos) + 1)


def ring_place(index, n):
    return jnp.where(index % 2 == 0, index // 2, n - 1 - index // 2)


def greet(axis, peers):
    barrier = pltpu.get_barrier_semaphore()
    for peer in peers:
        pl.semaphore_signal(barrier, inc=1, device_id={axis: peer}, device_id_type=MESH)
    pl.semaphore_wait(barrier, len(peers))


def cuts(columns, parts):
    lanes = columns // LANE
    sizes = [(lanes // parts + (1 if i < lanes % parts else 0)) * LANE for i in range(parts)]
    starts = [sum(sizes[:i]) for i in range(parts)]
    return list(zip(starts, sizes))


def ring_gather_kernel(n, axis, x_ref, o_ref, own_sem, send_sem, recv_sem):
    me = lax.axis_index(axis)
    pos = ring_place(me, n)
    right = ring_index((pos + 1) % n, n)
    left = ring_index((pos + n - 1) % n, n)
    greet(axis, (left, right))
    own = pltpu.make_async_copy(x_ref, o_ref.at[me], own_sem)
    own.start()
    pieces = cuts(x_ref.shape[1], 2)
    steps = n // 2
    sent = {}
    for step in range(steps):
        for part, (start, size) in enumerate(pieces):
            for way in range(2):
                if step == steps - 1 and part != way:
                    continue
                shift = n - step if way == 0 else step
                block = ring_index((pos + shift) % n, n)
                columns = pl.ds(start, size)
                if step > 0:
                    sent[(step - 1, part, way)].wait_recv()
                source = x_ref.at[:, columns] if step == 0 else o_ref.at[block, :, columns]
                copy = pltpu.make_async_remote_copy(
                    src_ref=source,
                    dst_ref=o_ref.at[block, :, columns],
                    send_sem=send_sem.at[step, part, way],
                    recv_sem=recv_sem.at[step, part, way],
                    device_id={axis: right if way == 0 else left},
                    device_id_type=MESH,
                )
                copy.start()
                sent[(step, part, way)] = copy
    for (step, part, way), copy in sent.items():
        if (step + 1, part, way) not in sent:
            copy.wait_recv()
    for copy in sent.values():
        copy.wait_send()
    own.wait()


def ring_gather(x, axis, ident):
    n = lax.axis_size(axis)
    return pl.pallas_call(
        functools.partial(ring_gather_kernel, n, axis),
        out_shape=jax.ShapeDtypeStruct((n,) + x.shape, x.dtype),
        in_specs=[pl.BlockSpec(memory_space=pltpu.VMEM)],
        out_specs=pl.BlockSpec(memory_space=pl.ANY),
        scratch_shapes=[
            pltpu.SemaphoreType.DMA,
            pltpu.SemaphoreType.DMA((n // 2, 2, 2)),
            pltpu.SemaphoreType.DMA((n // 2, 2, 2)),
        ],
        compiler_params=pltpu.CompilerParams(collective_id=ident, has_side_effects=True),
    )(x)


def ring_sum_kernel(n, axis, g_ref, o_ref, held, send_sem, recv_sem):
    me = lax.axis_index(axis)
    pos = ring_place(me, n)
    right = ring_index((pos + 1) % n, n)
    left = ring_index((pos + n - 1) % n, n)
    greet(axis, (left, right))
    pieces = cuts(g_ref.shape[2], 4)

    def copy_of(step, part, source):
        way = part % 2
        start, size = pieces[part]
        return pltpu.make_async_remote_copy(
            src_ref=source,
            dst_ref=held.at[step, :, pl.ds(start, size)],
            send_sem=send_sem.at[step, part],
            recv_sem=recv_sem.at[step, part],
            device_id={axis: right if way == 0 else left},
            device_id_type=MESH,
        )

    def block_of(step, part):
        shift = 2 * n - 1 - step if part % 2 == 0 else 1 + step
        return ring_index((pos + shift) % n, n)

    for part, (start, size) in enumerate(pieces):
        copy_of(0, part, g_ref.at[block_of(0, part), :, pl.ds(start, size)]).start()

    def one(step, carry):
        for part, (start, size) in enumerate(pieces):
            columns = pl.ds(start, size)
            slot = held.at[step - 1, :, columns]
            copy_of(step - 1, part, slot).wait_recv()
            held[step - 1, :, columns] = (
                held[step - 1, :, columns].astype(jnp.float32)
                + g_ref[block_of(step, part), :, columns].astype(jnp.float32)
            ).astype(held.dtype)
            copy_of(step, part, slot).start()
        return carry

    lax.fori_loop(1, n - 1, one, 0)
    for part, (start, size) in enumerate(pieces):
        columns = pl.ds(start, size)
        copy_of(n - 2, part, held.at[n - 2, :, columns]).wait_recv()
        o_ref[:, columns] = held[n - 2, :, columns].astype(jnp.float32) + g_ref[
            me, :, columns
        ].astype(jnp.float32)

    def drain(step, carry):
        for part, (start, size) in enumerate(pieces):
            copy_of(step, part, held.at[step, :, pl.ds(start, size)]).wait_send()
        return carry

    lax.fori_loop(0, n - 1, drain, 0)


def ring_sum(g, axis, ident):
    n, rows, columns = g.shape
    return pl.pallas_call(
        functools.partial(ring_sum_kernel, n, axis),
        out_shape=jax.ShapeDtypeStruct((rows, columns), jnp.float32),
        in_specs=[pl.BlockSpec(memory_space=pltpu.VMEM)],
        out_specs=pl.BlockSpec(memory_space=pltpu.VMEM),
        scratch_shapes=[
            pltpu.VMEM((n - 1, rows, columns), g.dtype),
            pltpu.SemaphoreType.DMA((n - 1, 4)),
            pltpu.SemaphoreType.DMA((n - 1, 4)),
        ],
        compiler_params=pltpu.CompilerParams(collective_id=ident, has_side_effects=True),
    )(g)


def gather_kernel(n, axis, x_ref, o_ref, send_sem, recv_sem):
    me = lax.axis_index(axis)
    peers = [(me + k) % n for k in range(1, n)]
    greet(axis, peers)
    copies = []
    for k, peer in enumerate(peers):
        copy = pltpu.make_async_remote_copy(
            src_ref=x_ref,
            dst_ref=o_ref.at[me],
            send_sem=send_sem.at[k],
            recv_sem=recv_sem.at[k],
            device_id={axis: peer},
            device_id_type=MESH,
        )
        copy.start()
        copies.append(copy)
    o_ref[me] = x_ref[...]
    for copy in copies:
        copy.wait()


def gather(x, axis, ident):
    n = lax.axis_size(axis)
    return pl.pallas_call(
        functools.partial(gather_kernel, n, axis),
        out_shape=jax.ShapeDtypeStruct((n,) + x.shape, x.dtype),
        in_specs=[pl.BlockSpec(memory_space=pltpu.VMEM)],
        out_specs=pl.BlockSpec(memory_space=pltpu.VMEM),
        scratch_shapes=[
            pltpu.SemaphoreType.DMA((n - 1,)),
            pltpu.SemaphoreType.DMA((n - 1,)),
        ],
        compiler_params=pltpu.CompilerParams(collective_id=ident, has_side_effects=True),
    )(x)


def scatter_sum_kernel(n, axis, x_ref, o_ref, held, send_sem, recv_sem):
    me = lax.axis_index(axis)
    peers = [(me + k) % n for k in range(1, n)]
    greet(axis, peers)
    copies = []
    for k, peer in enumerate(peers):
        copy = pltpu.make_async_remote_copy(
            src_ref=x_ref.at[peer],
            dst_ref=held.at[k],
            send_sem=send_sem.at[k],
            recv_sem=recv_sem.at[k],
            device_id={axis: peer},
            device_id_type=MESH,
        )
        copy.start()
        copies.append(copy)
    for copy in copies:
        copy.wait()
    total = x_ref[me].astype(jnp.float32)
    for k in range(n - 1):
        total = total + held[k].astype(jnp.float32)
    o_ref[...] = total


def scatter_sum(x, axis, ident):
    n = lax.axis_size(axis)
    rows, columns = x.shape[0] // n, x.shape[1]
    return pl.pallas_call(
        functools.partial(scatter_sum_kernel, n, axis),
        out_shape=jax.ShapeDtypeStruct((rows, columns), jnp.float32),
        in_specs=[pl.BlockSpec(memory_space=pltpu.VMEM)],
        out_specs=pl.BlockSpec(memory_space=pltpu.VMEM),
        scratch_shapes=[
            pltpu.VMEM((n - 1, rows, columns), x.dtype),
            pltpu.SemaphoreType.DMA((n - 1,)),
            pltpu.SemaphoreType.DMA((n - 1,)),
        ],
        compiler_params=pltpu.CompilerParams(collective_id=ident, has_side_effects=True),
    )(x.reshape(n, rows, columns))


def chain(decay, state, first, last, backward, ident):
    n = lax.axis_size("shard")
    me = lax.axis_index("shard")
    lines = jnp.zeros((16, DV), jnp.float32)
    lines = lines.at[0, :DK].set(decay).at[1, 0].set(first).at[1, 1].set(last)
    block = jnp.concatenate([state, lines], axis=0).astype(jnp.bfloat16)
    every = gather(block, "shard", ident)
    states = every[:, :DK].astype(jnp.float32)
    decays = every[:, DK, :DK].astype(jnp.float32)
    firsts = every[:, DK + 1, 0].astype(jnp.float32)
    lasts = every[:, DK + 1, 1].astype(jnp.float32)
    place = jnp.arange(n)
    j, i = place[:, None], place[None, :]
    if backward:
        passing = decays
        between = jnp.logical_and(i > me, i < j)
        counted = place > me
    else:
        before = jnp.concatenate([jnp.zeros((1,), jnp.float32), lasts[:-1]])
        passing = decays * (firsts == before).astype(jnp.float32)[:, None]
        between = jnp.logical_and(i > j, i < me)
        counted = place < me
    weight = jnp.prod(jnp.where(between[:, :, None], passing[None], 1.0), axis=1)
    weight = jnp.where(counted[:, None], weight, 0.0)
    incoming = jnp.sum(weight[:, :, None] * states, axis=0)
    prior = jnp.sum(jnp.where(place == me - 1, lasts, 0.0))
    return incoming[None], prior


def rms_scale(values):
    return lax.rsqrt(jnp.mean(values * values, axis=-1, keepdims=True) + EPS)


def group_pass(query, key, value_rows, logdec, segf, state, carry_seg):
    total = query.shape[0]
    heads = query.shape[1]
    count = total // GROUP
    scale = DK ** (-0.5)
    order = jnp.arange(GROUP)
    causal = order[:, None] >= order[None, :]

    def blocks(array):
        return array.reshape((count, GROUP) + array.shape[1:])

    def advance(carry, pieces):
        memory_state, prior = carry
        query_c, key_c, value_segment, decay_c, seg_c = pieces
        cumul = jnp.cumsum(decay_c, axis=0)
        query_decayed = query_c * jnp.exp(cumul) * scale
        key_inc = key_c * jnp.exp(-cumul)
        scores = jnp.einsum("thk,shk->hts", query_decayed, key_inc, precision=HIGH_PRECISION)
        joined = jnp.logical_and(causal, seg_c[:, None] == seg_c[None, :])
        scores = jnp.where(joined[None], scores, 0.0)
        inherit = (seg_c == prior).astype(jnp.float32)
        inside = jnp.einsum("hts,shv->thv", scores, value_segment, precision=HIGH_PRECISION)
        carried_state = jnp.einsum(
            "zsb,sbi->zsi", query_decayed, memory_state, precision=HIGH_PRECISION
        )
        result = inside + inherit[:, None, None] * carried_state
        final_result = cumul[-1]
        keep = (seg_c == seg_c[-1]).astype(jnp.float32)
        key_final_rows = key_c * jnp.exp(final_result[None] - cumul) * keep[:, None, None]
        linked_states = (seg_c[-1] == prior).astype(jnp.float32)
        memory_state = linked_states * jnp.exp(final_result)[
            :, :, None
        ] * memory_state + jnp.einsum(
            "zie,zir->ier", key_final_rows, value_segment, precision=HIGH_PRECISION
        )
        return ((memory_state, seg_c[-1]), result)

    (memory_state, last_seg), outs = lax.scan(
        advance,
        (state, carry_seg),
        (blocks(query), blocks(key), blocks(value_rows), blocks(logdec), blocks(segf)),
        unroll=True,
    )
    return (outs.reshape(total, heads, outs.shape[-1]), memory_state)


def on_device(
    resid_in,
    cotangent,
    segment,
    attn_gain,
    w_query,
    w_key,
    w_value,
    w_outgate,
    w_low,
    w_rank,
    rank_bias,
    head_gain,
    w_out,
    mlp_gain,
    w_gate,
    w_up,
    w_down,
):

    n = lax.axis_size("shard")
    wide = w_gate.shape[1]
    rows = w_query.shape[0]

    def tall(a):
        a = a.reshape(a.shape[0], -1)
        return jnp.pad(a, ((0, rows - a.shape[0]), (0, 0)))

    packed = jnp.concatenate(
        [
            w_query,
            w_key,
            w_value,
            w_outgate,
            w_out.T,
            w_gate,
            w_up,
            w_down.T,
            w_low,
            tall(attn_gain),
            tall(mlp_gain),
            tall(head_gain),
            tall(w_rank[:, 0, :].T),
            tall(rank_bias[0]),
        ],
        axis=1,
    )
    used = packed.shape[1]
    packed = jnp.pad(packed, ((0, 0), (0, -used % LANE)))
    every = ring_gather(packed, "shard", 1)
    spread = every.reshape(n * rows, packed.shape[1])
    edge_out = 2 * DK + 2 * DV
    edge_gate = edge_out + DV
    edge_down = edge_gate + 2 * wide
    edge_low = edge_down + wide
    project_w = spread[:, :edge_out]
    out_wt = spread[:, edge_out:edge_gate]
    gu_w = spread[:, edge_gate:edge_down]
    down_wt = spread[:, edge_down:edge_low]
    tail = every[:, :, edge_low:]
    low_w = tail[:, :, :GATE_RANK].reshape(D, GATE_RANK)
    gain_attn = tail[:, :, GATE_RANK].reshape(D).astype(jnp.float32)
    gain_mlp = tail[:, :, GATE_RANK + 1].reshape(D).astype(jnp.float32)
    gain_head = tail[:, : DV // n, GATE_RANK + 2].reshape(DV).astype(jnp.float32)
    rank_w = tail[:, : DK // n, GATE_RANK + 3 : 2 * GATE_RANK + 3].reshape(DK, GATE_RANK).T
    bias_w = tail[:, : DK // n, 2 * GATE_RANK + 3].reshape(DK)
    length = segment.shape[0]
    local_heads = 1
    scale = DK ** (-0.5)
    inv_attn = rms_scale(resid_in)
    normed_rows = (resid_in * inv_attn * gain_attn).astype(jnp.bfloat16)
    cot_rows = cotangent.astype(jnp.bfloat16)
    both = gather(jnp.concatenate([normed_rows, cot_rows], axis=1), "head", 2)
    normed_in = both[:, :, :D].reshape(length, D)
    cot_bf = both[:, :, D:].reshape(length, D)
    projected = jnp.dot(normed_in, project_w, preferred_element_type=jnp.float32)
    query = projected[:, :DK].reshape(length, local_heads, DK)
    key = projected[:, DK : 2 * DK].reshape(length, local_heads, DK)
    value_rows = projected[:, 2 * DK : 2 * DK + DV].reshape(length, local_heads, DV)
    outgate = projected[:, 2 * DK + DV :].reshape(length, local_heads, DV)
    low = jnp.dot(normed_in, low_w, preferred_element_type=jnp.float32)
    rank_mat = rank_w.astype(jnp.float32).reshape(GATE_RANK, local_heads * DK)
    logit = jnp.dot(low, rank_mat, precision=HIGH_PRECISION) + bias_w.astype(jnp.float32).reshape(
        local_heads * DK
    )
    logdec = (jax.nn.log_sigmoid(logit) / 16.0).reshape(length, local_heads, DK)
    segf = segment.astype(jnp.float32) + 1.0
    first_seg = segf[:1]
    last_seg = segf[-1:]
    cumul = jnp.cumsum(logdec, axis=0)
    keep = (segf == last_seg[0]).astype(jnp.float32)
    key_final_rows = key * jnp.exp(cumul[-1][None] - cumul) * keep[:, None, None]
    summary_state = jnp.einsum("zie,zir->ier", key_final_rows, value_rows, precision=HIGH_PRECISION)
    through = jnp.exp(cumul[-1]) * (first_seg[0] == last_seg[0]).astype(jnp.float32)
    state_in, prior = chain(through[0], summary_state[0], first_seg[0], last_seg[0], False, 3)

    def mixer(query_in, key_in, value_in, decay_in):
        return group_pass(query_in, key_in, value_in, decay_in, segf, state_in, prior)

    (mixed, state_out), mixer_back = jax.vjp(mixer, query, key, value_rows, logdec)
    inv_head = rms_scale(mixed)
    headnormed = mixed * inv_head * gain_head
    sigma_out = jax.nn.sigmoid(outgate)
    swish_out = outgate * sigma_out
    gated = (headnormed * swish_out).reshape(length, local_heads * DV).astype(jnp.bfloat16)
    resid_mid = resid_in + scatter_sum(
        jnp.dot(gated, out_wt.T, preferred_element_type=jnp.float32).astype(jnp.bfloat16),
        "head",
        4,
    )
    inv_mlp = rms_scale(resid_mid)
    mid_rows = (resid_mid * inv_mlp * gain_mlp).astype(jnp.bfloat16)
    normed_mid = gather(mid_rows, "head", 5).reshape(length, D)
    gate_up = jnp.dot(normed_mid, gu_w, preferred_element_type=jnp.float32)
    gate_pre = gate_up[:, :wide]
    up_pre = gate_up[:, wide:]
    sigma_gate = jax.nn.sigmoid(gate_pre)
    active = gate_pre * sigma_gate
    hidden = (active * up_pre).astype(jnp.bfloat16)
    d_hidden = jnp.dot(cot_bf, down_wt, preferred_element_type=jnp.float32)
    d_gatepre = (d_hidden * up_pre * sigma_gate * (1.0 + gate_pre * (1.0 - sigma_gate))).astype(
        jnp.bfloat16
    )
    d_uppre = (d_hidden * active).astype(jnp.bfloat16)
    d_gu = jnp.concatenate([d_gatepre, d_uppre], axis=1)
    grad_down = jnp.dot(cot_bf.T, hidden, preferred_element_type=jnp.float32)
    grad_gu = jnp.dot(normed_mid.T, d_gu, preferred_element_type=jnp.float32)
    shares = jnp.concatenate(
        [
            jnp.dot(hidden, down_wt.T, preferred_element_type=jnp.float32).astype(jnp.bfloat16),
            jnp.dot(d_gu, gu_w.T, preferred_element_type=jnp.float32).astype(jnp.bfloat16),
        ],
        axis=1,
    )
    summed = scatter_sum(shares, "head", 6)
    resid_out = resid_mid + summed[:, :D]
    d_normmid = summed[:, D:]
    part_mlp_gain = jnp.sum(d_normmid * resid_mid * inv_mlp, axis=0)
    scaled_mid = gain_mlp * d_normmid
    d_mid = (
        cotangent
        + inv_mlp * scaled_mid
        - resid_mid * inv_mlp**3 * jnp.mean(scaled_mid * resid_mid, axis=-1, keepdims=True)
    )
    dmid_rows = d_mid.astype(jnp.bfloat16)
    dmid_bf = gather(dmid_rows, "head", 7).reshape(length, D)
    d_gated = jnp.dot(dmid_bf, out_wt, preferred_element_type=jnp.float32).reshape(
        length, local_heads, DV
    )
    grad_out = jnp.dot(dmid_bf.T, gated, preferred_element_type=jnp.float32)
    d_head = d_gated * swish_out
    d_outgate = (
        (d_gated * headnormed * sigma_out * (1.0 + outgate * (1.0 - sigma_out)))
        .reshape(length, local_heads * DV)
        .astype(jnp.bfloat16)
    )
    part_head_gain = jnp.sum(d_head * mixed * inv_head, axis=(0, 1))
    scaled_head = gain_head * d_head
    mixed_gradient = inv_head * scaled_head - mixed * inv_head**3 * jnp.mean(
        scaled_head * mixed, axis=-1, keepdims=True
    )
    inherit = (segf == prior).astype(jnp.float32)
    weighted_query = query * jnp.exp(cumul) * inherit[:, None, None] * scale
    local_gradient = jnp.einsum(
        "zie,zir->ier", weighted_query, mixed_gradient, precision=HIGH_PRECISION
    )
    through_all = jnp.exp(cumul[-1]) * (last_seg[0] == prior).astype(jnp.float32)
    nothing = jnp.zeros((), jnp.float32)
    outgoing, _ = chain(through_all[0], local_gradient[0], nothing, nothing, True, 8)
    d_query, d_key, d_value, d_logdec = mixer_back((mixed_gradient, outgoing))
    query_bf = d_query.reshape(length, local_heads * DK).astype(jnp.bfloat16)
    key_bf = d_key.reshape(length, local_heads * DK).astype(jnp.bfloat16)
    value_bf = d_value.reshape(length, local_heads * DV).astype(jnp.bfloat16)
    d_logit = d_logdec.reshape(length, local_heads * DK) * jax.nn.sigmoid(-logit) / 16.0
    grad_bias = jnp.sum(d_logit, axis=0).reshape(local_heads, DK)
    grad_rank = jnp.dot(low.T, d_logit, precision=HIGH_PRECISION).reshape(
        GATE_RANK, local_heads, DK
    )
    d_low = (
        jnp.einsum(
            "thk,rhk->thr",
            d_logit.reshape(length, local_heads, DK),
            rank_w.astype(jnp.float32).reshape(GATE_RANK, local_heads, DK),
            precision=HIGH_PRECISION,
        )
        .astype(jnp.bfloat16)
        .reshape(length, local_heads * GATE_RANK)
    )
    part_low = (
        jnp.dot(normed_in.T, d_low, preferred_element_type=jnp.float32)
        .reshape(D, local_heads, GATE_RANK)
        .sum(axis=1)
    )
    d_project = jnp.concatenate([query_bf, key_bf, value_bf, d_outgate], axis=1)
    grad_project = jnp.dot(normed_in.T, d_project, preferred_element_type=jnp.float32)
    low_rows = low_w.T
    total_term = jnp.dot(d_project, project_w.T, preferred_element_type=jnp.float32)
    d_normin = scatter_sum(
        (total_term + jnp.dot(d_low, low_rows, preferred_element_type=jnp.float32)).astype(
            jnp.bfloat16
        ),
        "head",
        9,
    )
    part_attn_gain = jnp.sum(d_normin * resid_in * inv_attn, axis=0)
    scaled_in = gain_attn * d_normin
    grad_in = (
        d_mid
        + inv_attn * scaled_in
        - resid_in * inv_attn**3 * jnp.mean(scaled_in * resid_in, axis=-1, keepdims=True)
    )

    def owners(a):
        a = a.reshape(n, a.shape[0] // n, -1)
        return jnp.pad(a, ((0, 0), (0, rows - a.shape[1]), (0, 0))).reshape(D, -1)

    grads = jnp.concatenate(
        [
            g.astype(jnp.bfloat16)
            for g in (
                grad_project,
                grad_out,
                grad_gu,
                grad_down,
                part_low,
                part_attn_gain[:, None],
                part_mlp_gain[:, None],
                owners(part_head_gain),
                owners(grad_rank[:, 0, :].T),
                owners(grad_bias[0]),
            )
        ],
        axis=1,
    )
    grads = jnp.pad(grads, ((0, 0), (0, packed.shape[1] - used)))
    owned = ring_sum(grads.reshape(n, rows, packed.shape[1]), "shard", 10)
    heads = lax.axis_size("head")
    shared = owned[:, edge_low : edge_low + GATE_RANK + 3]
    gain_rows = DV // n
    final_rank = owned[: DK // n, edge_low + GATE_RANK + 3 : edge_low + 2 * GATE_RANK + 3]
    final_bias = owned[: DK // n, edge_low + 2 * GATE_RANK + 3]
    shares = jnp.concatenate(
        [
            shared[:, : GATE_RANK + 2].reshape(heads, rows // heads, GATE_RANK + 2),
            jnp.pad(
                shared[:gain_rows, GATE_RANK + 2].reshape(heads, gain_rows // heads, 1),
                ((0, 0), (0, (rows - gain_rows) // heads), (0, 0)),
            ),
        ],
        axis=2,
    )
    deep = max(rows // heads, 16)
    shares = jnp.pad(
        shares, ((0, 0), (0, deep - rows // heads), (0, LANE - GATE_RANK - 3))
    ).reshape(heads * deep, LANE)
    final = scatter_sum(shares.astype(jnp.bfloat16), "head", 11)[: rows // heads]
    return (
        resid_out,
        grad_in,
        final[:, GATE_RANK],
        owned[:, :DK],
        owned[:, DK : 2 * DK],
        owned[:, 2 * DK : 2 * DK + DV],
        owned[:, 2 * DK + DV : edge_out],
        final[:, :GATE_RANK],
        final_rank.T.reshape(GATE_RANK, 1, DK // n),
        final_bias.reshape(1, DK // n),
        final[: gain_rows // heads, GATE_RANK + 2],
        owned[:, edge_out:edge_gate].T,
        final[:, GATE_RANK + 1],
        owned[:, edge_gate : edge_gate + wide],
        owned[:, edge_gate + wide : edge_down],
        owned[:, edge_down:edge_low].T,
    )


def solution(mesh):
    in_specs = (
        P(("shard", "head"), None),
        P(("shard", "head"), None),
        P("shard"),
        P("shard"),
        P("shard", "head"),
        P("shard", "head"),
        P("shard", "head"),
        P("shard", "head"),
        P("shard", None),
        P(None, "head", "shard"),
        P("head", "shard"),
        P("shard"),
        P("head", "shard"),
        P("shard"),
        P("shard", "head"),
        P("shard", "head"),
        P("head", "shard"),
    )
    out_specs = (
        P(("shard", "head"), None),
        P(("shard", "head"), None),
        P(("shard", "head")),
        P("shard", "head"),
        P("shard", "head"),
        P("shard", "head"),
        P("shard", "head"),
        P(("shard", "head"), None),
        P(None, "head", "shard"),
        P("head", "shard"),
        P(("shard", "head")),
        P("head", "shard"),
        P(("shard", "head")),
        P("shard", "head"),
        P("shard", "head"),
        P("head", "shard"),
    )
    return jax.shard_map(
        on_device, mesh=mesh, in_specs=in_specs, out_specs=out_specs, check_vma=False
    )
```

time: 1550 us -> 417 us (0.27)
  waiting for transfers between devices: 884 us -> 0 us
  blocking collectives: 455 us -> 0 us
  Pallas kernels: 0 us -> 254 us
  loops' own time: 19.8 us -> 0 us
  matrix products: 60.1 us -> 43.8 us
    reduce_scatter x12 -> x0, waiting for transfers between devices: 555 us -> none  [the longest x1 76.3 us: on_device(): lax.psum_scatter(grad_down, 'shard', scatter_dimension=1, tiled=True)]
    all_gather x17 -> x0, blocking collectives: 392 us -> none  [the longest x4 99.5 us: entering(): lax.all_gather(a.astype(kind), axis)]
    pallas_call x0 -> x11, Pallas kernels: none -> 254 us  [the longest x1 76.2 us: ring_sum(): pl.pallas_call(functools.partial(ring_sum_kernel, n, axis), out_shape=jax...]
    unnamed x21 -> x0, waiting for transfers between devices: 241 us -> none
    all_gather x3 -> x0, waiting for transfers between devices: 87.1 us -> none  [the longest x1 40 us: fetch(): lax.all_gather(w_down, 'shard', axis=1, tiled=True)]
    unnamed x2 -> x0, blocking collectives: 63.3 us -> none
    dynamic_slice x47 -> x0, local copies, waits for them, and re-layouts: 20.3 us -> none  [the longest x40 16.2 us: group_pass(): lax.scan(advance, (state, carry_seg), (blocks(query), blocks(key), blocks...]
    another operation x4 -> x0, loops' own time: 19.8 us -> none  [the longest x2 14 us: entering(): return lax.fori_loop(0, ahead, one, state)]
  transfers between devices with their start and end apart: 18 -> 0, of which waited for: 16 -> 0; matrix products, arithmetic and copies ran while one was open for 2% -> 0% of each run, Pallas kernels for 0% -> 0%
where the time goes in v1:
time: 417 us; the launch traced here: 414 us
  Pallas kernels  254 us (61%)
  local copies, waits for them, and re-layouts  62.7 us (15%)
  matrix products  43.8 us (11%)
  other arithmetic  43.1 us (10%)
  between operations  10.4 us (2%)
    pallas_call x1, Pallas kernels, ring_sum(): pl.pallas_call(functools.partial(ring_sum_kernel, n, axis), out_shape=jax...  76.2 us
    pallas_call x1, Pallas kernels, ring_gather(): pl.pallas_call(functools.partial(ring_gather_kernel, n, axis), out_shape=...  69.5 us
    pallas_call x5, Pallas kernels, gather(): pl.pallas_call(functools.partial(gather_kernel, n, axis), out_shape=jax.S...  68.4 us
    pallas_call x4, Pallas kernels, scatter_sum(): pl.pallas_call(functools.partial(scatter_sum_kernel, n, axis), out_shape=...  39.7 us
    unnamed x188, local copies, waits for them, and re-layouts  13.2 us
    concatenate x1, local copies, waits for them, and re-layouts, on_device(): jnp.concatenate([g.astype(jnp.bfloat16) for g in (grad_project, grad_out,...  10.7 us

profile of v1, /device:TPU:0, one launch (start us, length us, event | category | flops | bytes accessed | tf_op | source)
XLA Modules:
  0.0 413.8 jit_solution(6692726431451042873)
XLA Ops:
  23.7 69.5 %shard_map.288 = bf16[8,128,3200]{2,1,0:T(8,128)(2,1)} custom-call(bf16[128,3200]{1,0:T(8,128)(2,1)} %pad.86.x_ref), custom_call_target="tpu_custom_call" | custom-call | tf_op jit(solution)/shard_map/pallas_call | solution.py:87
  100.1 15.3 %shard_map.289 = bf16[4,64,2048]{2,1,0:T(8,128)(2,1)} custom-call(bf16[64,2048]{1,0:T(8,128)(2,1)} %pad_maximum_fusion.5.x_ref), custom_call_target="tpu_custom_call" | custom-call | tf_op jit(solution)/shard_map/pallas_call | solution.py:195
  121.3 2.0 fusion.10
  126.2 15.2 %shard_map.290 = bf16[8,144,256]{2,1,0:T(8,128)(2,1)} custom-call(bf16[144,256]{1,0:T(8,128)(2,1)} %pad_maximum_fusion.9.x_ref), custom_call_target="tpu_custom_call" | custom-call | tf_op jit(solution)/shard_map/pallas_call | solution.py:195
  146.9 3.9 compare_convert_fusion
  158.9 2.2 convolution_convert_fusion.4
  161.1 8.7 %shard_map.291 = f32[64,1024]{1,0:T(8,128)} custom-call(bf16[4,64,1024]{2,1,0:T(8,128)(2,1)} %bitcast.696), custom_call_target="tpu_custom_call" | custom-call | tf_op jit(solution)/shard_map/pallas_call | solution.py:235
  172.7 9.8 %shard_map.292 = bf16[4,64,1024]{2,1,0:T(8,128)(2,1)} custom-call(bf16[64,1024]{1,0:T(8,128)(2,1)} %multiply_convert_fusion.4.x_ref), custom_call_target="tpu_custom_call" | custom-call | tf_op jit(solution)/shard_map/pallas_call | solution.py:195
  182.5 3.1 fusion.2
  185.7 2.3 multiply_convert_fusion.1
  190.8 15.9 %shard_map.293 = f32[64,2048]{1,0:T(8,128)} custom-call(bf16[4,64,2048]{2,1,0:T(8,128)(2,1)} %bitcast.689), custom_call_target="tpu_custom_call" | custom-call | tf_op jit(solution)/shard_map/pallas_call | solution.py:235
  207.9 2.0 fusion.221
  210.8 9.8 %shard_map.294 = bf16[4,64,1024]{2,1,0:T(8,128)(2,1)} custom-call(bf16[64,1024]{1,0:T(8,128)(2,1)} %get-tuple-element.174.x_ref), custom_call_target="tpu_custom_call" | custom-call | tf_op jit(solution)/shard_map/pallas_call | solution.py:195
  222.0 2.8 fusion.70
  237.9 18.3 %shard_map.295 = bf16[8,144,256]{2,1,0:T(8,128)(2,1)} custom-call(bf16[144,256]{1,0:T(8,128)(2,1)} %pad_maximum_fusion.10.x_ref), custom_call_target="tpu_custom_call" | custom-call | tf_op jit(solution)/shard_map/pallas_call | solution.py:195
  273.4 2.9 fusion.15
  276.3 10.0 %shard_map.296 = f32[64,1024]{1,0:T(8,128)} custom-call(bf16[4,64,1024]{2,1,0:T(8,128)(2,1)} %bitcast.704), custom_call_target="tpu_custom_call" | custom-call | tf_op jit(solution)/shard_map/pallas_call | solution.py:235
  291.9 2.7 copy.242
  294.6 2.3 convolution_convert_fusion
  297.0 10.7 %concatenate.86 = bf16[1024,3172]{1,0:T(8,128)(2,1)} concatenate(bf16[1024,768]{1,0:T(8,128)(2,1)} %copy.242, bf16[1024,256]{1,0:T(8,128)(2,1)} %copy.243, bf16[1024,1408]{1,0:T(8,128)(2,1)S(1)} %convolution_convert_fusion, bf16[1024,704]{1,0:T(8,128)(2,1)} %copy.244, bf16[1024,16]{1,0:T(8,128)(2,1)} %copy.245, bf16[1024,1]{1,0:T(8,128)(2,1)} %convert_element_type.373, ...), dimensions={1} | concatenate | bytes 12992512 | tf_op jit(solution)/shard_map/concatenate | solution.py:544
  307.6 6.0 %pad.94 = bf16[1024,3200]{1,0:T(8,128)(2,1)} pad(bf16[1024,3172]{1,0:T(8,128)(2,1)} %concatenate.86, bf16[]{:T(256)} %constant.195.clone.1), padding=0_0x0_28 | pad | bytes 13049858 | tf_op jit(solution)/shard_map/jit(_pad)/pad | solution.py:562
  313.7 76.2 %shard_map.297 = f32[128,3200]{1,0:T(8,128)} custom-call(bf16[8,128,3200]{2,1,0:T(8,128)(2,1)} %bitcast.621), custom_call_target="tpu_custom_call" | custom-call | tf_op jit(solution)/shard_map/pallas_call | solution.py:158
  396.9 2.4 convert.121
  402.7 5.1 %shard_map.298 = f32[32,128]{1,0:T(8,128)} custom-call(bf16[4,32,128]{2,1,0:T(8,128)(2,1)} %pad.96.x_ref), custom_call_target="tpu_custom_call" | custom-call | tf_op jit(solution)/shard_map/pallas_call | solution.py:235
  (376 shorter events, 104.4 us)
Async XLA Ops:
  2.3 95.8 %copy-start.64 = (f32[64]{0:T(128)}, f32[64]{0:T(128)S(1)}, u32[]{:S(2)}) copy-start(f32[64]{0:T(128)S(1)} %get-tuple-element.229) | copy-start | bytes 772
  4.8 119.2 %copy-start.35 = (f32[64]{0:T(128)}, f32[64]{0:T(128)S(1)}, u32[]{:S(2)}) copy-start(f32[64]{0:T(128)S(1)} %get-tuple-element.219) | copy-start | bytes 772
  23.7 74.4 %copy-start.1 = (f32[64,1024]{1,0:T(8,128)S(1)}, f32[64,1024]{1,0:T(8,128)}, u32[]{:S(2)}) copy-start(f32[64,1024]{1,0:T(8,128)} %param.29) | copy-start | bytes 786436
  116.7 69.0 %copy-start.2 = (bf16[4,64,1024]{2,1,0:T(8,128)(2,1)}, bf16[4,64,1024]{2,1,0:T(8,128)(2,1)S(1)}, u32[]{:S(2)}) copy-start(bf16[4,64,1024]{2,1,0:T(8,128)(2,1)S(1)} %get-tuple-element.190) | copy-start | bytes 1572868
  118.2 27.4 %copy-start.5 = (f32[256,1,128]{2,0,1:T(8,128)}, f32[256,1,128]{2,0,1:T(8,128)S(1)}, u32[]{:S(2)}) copy-start(f32[256,1,128]{2,0,1:T(8,128)S(1)} %fusion.95) | copy-start | bytes 393220
  119.9 36.7 %copy-start.69 = (f32[128]{0:T(128)}, f32[128]{0:T(128)S(1)}, u32[]{:S(2)}) copy-start(f32[128]{0:T(128)S(1)} %exponential_multiply_fusion.1) | copy-start | bytes 1540
  121.1 35.5 %copy-start.53 = (f32[128]{0:T(128)}, f32[128]{0:T(128)S(1)}, u32[]{:S(2)}) copy-start(f32[128]{0:T(128)S(1)} %get-tuple-element.245) | copy-start | bytes 1540
  121.2 34.7 %copy-start.57 = (f32[128]{0:T(128)}, f32[128]{0:T(128)S(1)}, u32[]{:S(2)}) copy-start(f32[128]{0:T(128)S(1)} %slice_bitcast_fusion.10) | copy-start | bytes 1540
  121.2 34.7 %copy-start.71 = (f32[128]{0:T(128)}, f32[128]{0:T(128)S(1)}, u32[]{:S(2)}) copy-start(f32[128]{0:T(128)S(1)} %exponential_multiply_fusion.2) | copy-start | bytes 1540
  121.3 34.0 %copy-start.59 = (f32[128]{0:T(128)}, f32[128]{0:T(128)S(1)}, u32[]{:S(2)}) copy-start(f32[128]{0:T(128)S(1)} %slice_bitcast_fusion.11) | copy-start | bytes 1540
  123.3 29.3 %copy-start.74 = (pred[8,8]{1,0:T(8,128)(4,1)S(1)}, pred[8,8]{1,0:T(8,128)(4,1)}, u32[]{:S(2)}) copy-start(pred[8,8]{1,0:T(8,128)(4,1)} %fusion.199) | copy-start | bytes 196
  123.4 29.4 %copy-start.81 = (pred[8]{0:T(512)(128)(4,1)S(1)}, pred[8]{0:T(512)(128)(4,1)}, u32[]{:S(2)}) copy-start(pred[8]{0:T(512)(128)(4,1)} %copy-done.80) | copy-start | bytes 28
  123.6 32.4 %copy-start.16 = (f32[64,64]{1,0:T(8,128)}, f32[64,64]{1,0:T(8,128)S(1)}, u32[]{:S(2)}) copy-start(f32[64,64]{1,0:T(8,128)S(1)} %convolution_select_fusion.4) | copy-start | bytes 49156
  123.8 32.2 %copy-start.18 = (f32[64,64]{1,0:T(8,128)}, f32[64,64]{1,0:T(8,128)S(1)}, u32[]{:S(2)}) copy-start(f32[64,64]{1,0:T(8,128)S(1)} %convolution_select_fusion.5) | copy-start | bytes 49156
  124.0 32.4 %copy-start.12 = (f32[64,64]{1,0:T(8,128)}, f32[64,64]{1,0:T(8,128)S(1)}, u32[]{:S(2)}) copy-start(f32[64,64]{1,0:T(8,128)S(1)} %convolution_select_fusion.6) | copy-start | bytes 49156
  124.2 32.1 %copy-start.14 = (f32[64,64]{1,0:T(8,128)}, f32[64,64]{1,0:T(8,128)S(1)}, u32[]{:S(2)}) copy-start(f32[64,64]{1,0:T(8,128)S(1)} %convolution_select_fusion.7) | copy-start | bytes 49156
  228.4 28.6 %copy-start.73 = (pred[8,8]{1,0:T(8,128)(4,1)S(1)}, pred[8,8]{1,0:T(8,128)(4,1)}, u32[]{:S(2)}) copy-start(pred[8,8]{1,0:T(8,128)(4,1)} %fusion.200) | copy-start | bytes 196
  228.4 28.7 %copy-start.79 = (pred[8]{0:T(512)(128)(4,1)S(1)}, pred[8]{0:T(512)(128)(4,1)}, u32[]{:S(2)}) copy-start(pred[8]{0:T(512)(128)(4,1)} %copy-done.78) | copy-start | bytes 28
  234.5 24.0 %copy-start.52 = (f32[64]{0:T(128)S(1)}, f32[64]{0:T(128)}, u32[]{:S(2)}) copy-start(f32[64]{0:T(128)} %copy-done.50) | copy-start | bytes 772
  234.5 24.0 %copy-start.76 = (f32[128]{0:T(128)S(1)}, f32[128]{0:T(128)}, u32[]{:S(2)}) copy-start(f32[128]{0:T(128)} %exponential_multiply_fusion) | copy-start | bytes 1540
  234.9 24.1 %copy-start.49 = (f32[64]{0:T(128)S(1)}, f32[64]{0:T(128)}, u32[]{:S(2)}) copy-start(f32[64]{0:T(128)} %copy-done.47) | copy-start | bytes 772
  235.0 24.1 %copy-start.70 = (f32[128]{0:T(128)S(1)}, f32[128]{0:T(128)}, u32[]{:S(2)}) copy-start(f32[128]{0:T(128)} %copy-done.69) | copy-start | bytes 1540
  235.8 23.7 %copy-start.46 = (f32[64]{0:T(128)S(1)}, f32[64]{0:T(128)}, u32[]{:S(2)}) copy-start(f32[64]{0:T(128)} %copy-done.44) | copy-start | bytes 772
  235.8 23.7 %copy-start.72 = (f32[128]{0:T(128)S(1)}, f32[128]{0:T(128)}, u32[]{:S(2)}) copy-start(f32[128]{0:T(128)} %copy-done.71) | copy-start | bytes 1540
  (61 other events, 582.9 us)

commit v2 on v1

--- a/solution.py
+++ b/solution.py
@@ -28,11 +28,27 @@
     return jnp.where(index % 2 == 0, index // 2, n - 1 - index // 2)
 
 
-def greet(axis, peers):
+def greet(*pairs):
     barrier = pltpu.get_barrier_semaphore()
-    for peer in peers:
+    for axis, peer in pairs:
         pl.semaphore_signal(barrier, inc=1, device_id={axis: peer}, device_id_type=MESH)
-    pl.semaphore_wait(barrier, len(peers))
+    pl.semaphore_wait(barrier, len(pairs))
+
+
+def remote(source, target, send_sem, recv_sem, axis, peer):
+    return pltpu.make_async_remote_copy(
+        src_ref=source,
+        dst_ref=target,
+        send_sem=send_sem,
+        recv_sem=recv_sem,
+        device_id={axis: peer},
+        device_id_type=MESH,
+    )
+
+
+def quad(axis):
+    me = lax.axis_index(axis)
+    return me, me + 1 - 2 * (me % 2), (me + 2) % 4
 
 
 def cuts(columns, parts):
@@ -43,11 +59,20 @@
 
 
 def ring_gather_kernel(n, axis, x_ref, o_ref, own_sem, send_sem, recv_sem):
+    right, left = ring_sides(n, axis)
+    greet((axis, left), (axis, right))
+    ring_gather_body(n, axis, x_ref, o_ref, own_sem, send_sem, recv_sem, None)
+
+
+def ring_sides(n, axis):
+    pos = ring_place(lax.axis_index(axis), n)
+    return ring_index((pos + 1) % n, n), ring_index((pos + n - 1) % n, n)
+
+
+def ring_gather_body(n, axis, x_ref, o_ref, own_sem, send_sem, recv_sem, meanwhile):
     me = lax.axis_index(axis)
     pos = ring_place(me, n)
-    right = ring_index((pos + 1) % n, n)
-    left = ring_index((pos + n - 1) % n, n)
-    greet(axis, (left, right))
+    right, left = ring_sides(n, axis)
     own = pltpu.make_async_copy(x_ref, o_ref.at[me], own_sem)
     own.start()
     pieces = cuts(x_ref.shape[1], 2)
@@ -74,6 +99,8 @@
                 )
                 copy.start()
                 sent[(step, part, way)] = copy
+        if step == 0 and meanwhile is not None:
+            meanwhile()
     for (step, part, way), copy in sent.items():
         if (step + 1, part, way) not in sent:
             copy.wait_recv()
@@ -98,152 +125,244 @@
     )(x)
 
 
-def ring_sum_kernel(n, axis, g_ref, o_ref, held, send_sem, recv_sem):
+def quad_gather_parts(axis, x_ref, o_ref, send_sem, recv_sem):
+    me, beside, across = quad(axis)
+    half = x_ref.shape[0] // 2
+    parts = [pl.ds(0, half), pl.ds(half, half)]
+    first = [
+        (
+            remote(x_ref.at[rows], o_ref.at[me, rows], send_sem.at[i, 0], recv_sem.at[i, 0], axis, across),
+            remote(x_ref.at[rows], o_ref.at[me, rows], send_sem.at[i, 1], recv_sem.at[i, 1], axis, beside),
+        )
+        for i, rows in enumerate(parts)
+    ]
+    onward = [
+        remote(
+            o_ref.at[across, rows],
+            o_ref.at[across, rows],
+            send_sem.at[i, 2],
+            recv_sem.at[i, 2],
+            axis,
+            beside,
+        )
+        for i, rows in enumerate(parts)
+    ]
+
+    def start():
+        for far, near in first:
+            far.start()
+            near.start()
+        o_ref[me] = x_ref[...]
+
+    def relay():
+        for (far, _), more in zip(first, onward):
+            far.wait_recv()
+            more.start()
+
+    def finish():
+        for (far, near), more in zip(first, onward):
+            near.wait_recv()
+            more.wait_recv()
+            far.wait_send()
+            near.wait_send()
+            more.wait_send()
+
+    return start, relay, finish
+
+
+def gather_kernel(axis, x_ref, o_ref, send_sem, recv_sem):
+    _, beside, across = quad(axis)
+    greet((axis, beside), (axis, across))
+    start, relay, finish = quad_gather_parts(axis, x_ref, o_ref, send_sem, recv_sem)
+    start()
+    relay()
+    finish()
+
+
+def gather(x, axis, ident):
+    return pl.pallas_call(
+        functools.partial(gather_kernel, axis),
+        out_shape=jax.ShapeDtypeStruct((4,) + x.shape, x.dtype),
+        in_specs=[pl.BlockSpec(memory_space=pltpu.VMEM)],
+        out_specs=pl.BlockSpec(memory_space=pltpu.VMEM),
+        scratch_shapes=[
+            pltpu.SemaphoreType.DMA((2, 3)),
+            pltpu.SemaphoreType.DMA((2, 3)),
+        ],
+        compiler_params=pltpu.CompilerParams(collective_id=ident, has_side_effects=True),
+    )(x)
+
+
+def enter_kernel(n, w_ref, x_ref, spread_ref, o_ref, own_sem, send_w, recv_w, send_x, recv_x):
+    right, left = ring_sides(n, "shard")
+    _, beside, across = quad("head")
+    greet(("shard", left), ("shard", right), ("head", beside), ("head", across))
+    start, relay, finish = quad_gather_parts("head", x_ref, o_ref, send_x, recv_x)
+    start()
+    ring_gather_body(n, "shard", w_ref, spread_ref, own_sem, send_w, recv_w, relay)
+    finish()
+
+
+def enter(weights, x, ident):
+    n = lax.axis_size("shard")
+    return pl.pallas_call(
+        functools.partial(enter_kernel, n),
+        out_shape=(
+            jax.ShapeDtypeStruct((n,) + weights.shape, weights.dtype),
+            jax.ShapeDtypeStruct((4,) + x.shape, x.dtype),
+        ),
+        in_specs=[pl.BlockSpec(memory_space=pltpu.VMEM)] * 2,
+        out_specs=(
+            pl.BlockSpec(memory_space=pl.ANY),
+            pl.BlockSpec(memory_space=pltpu.VMEM),
+        ),
+        scratch_shapes=[
+            pltpu.SemaphoreType.DMA,
+            pltpu.SemaphoreType.DMA((n // 2, 2, 2)),
+            pltpu.SemaphoreType.DMA((n // 2, 2, 2)),
+            pltpu.SemaphoreType.DMA((2, 3)),
+            pltpu.SemaphoreType.DMA((2, 3)),
+        ],
+        compiler_params=pltpu.CompilerParams(collective_id=ident, has_side_effects=True),
+    )(weights, x)
+
+
+def ring_sum_kernel(n, axis, pieces, count, *refs):
+    g_refs, o_refs = refs[:count], refs[count : 2 * count]
+    held, send_sem, recv_sem = refs[2 * count :]
     me = lax.axis_index(axis)
     pos = ring_place(me, n)
-    right = ring_index((pos + 1) % n, n)
-    left = ring_index((pos + n - 1) % n, n)
-    greet(axis, (left, right))
-    pieces = cuts(g_ref.shape[2], 4)
+    right, left = ring_sides(n, axis)
+    greet((axis, left), (axis, right))
+
+    def slot_of(step, part):
+        start, size = pieces[part][3:]
+        return held.at[step, :, pl.ds(start, size)]
 
     def copy_of(step, part, source):
-        way = part % 2
-        start, size = pieces[part]
-        return pltpu.make_async_remote_copy(
-            src_ref=source,
-            dst_ref=held.at[step, :, pl.ds(start, size)],
-            send_sem=send_sem.at[step, part],
-            recv_sem=recv_sem.at[step, part],
-            device_id={axis: right if way == 0 else left},
-            device_id_type=MESH,
-        )
-
-    def block_of(step, part):
-        shift = 2 * n - 1 - step if part % 2 == 0 else 1 + step
-        return ring_index((pos + shift) % n, n)
-
-    for part, (start, size) in enumerate(pieces):
-        copy_of(0, part, g_ref.at[block_of(0, part), :, pl.ds(start, size)]).start()
+        return remote(
+            source,
+            slot_of(step, part),
+            send_sem.at[step, part],
+            recv_sem.at[step, part],
+            axis,
+            right if pieces[part][1] == 0 else left,
+        )
+
+    def own_of(step, part):
+        which, way, start, _, size = pieces[part]
+        shift = 2 * n - 1 - step if way == 0 else 1 + step
+        return g_refs[which].at[ring_index((pos + shift) % n, n), :, pl.ds(start, size)]
+
+    for part in range(len(pieces)):
+        copy_of(0, part, own_of(0, part)).start()
 
     def one(step, carry):
-        for part, (start, size) in enumerate(pieces):
-            columns = pl.ds(start, size)
-            slot = held.at[step - 1, :, columns]
+        for part in range(len(pieces)):
+            slot = slot_of(step - 1, part)
             copy_of(step - 1, part, slot).wait_recv()
-            held[step - 1, :, columns] = (
-                held[step - 1, :, columns].astype(jnp.float32)
-                + g_ref[block_of(step, part), :, columns].astype(jnp.float32)
+            slot[...] = (
+                slot[...].astype(jnp.float32) + own_of(step, part)[...].astype(jnp.float32)
             ).astype(held.dtype)
             copy_of(step, part, slot).start()
         return carry
 
     lax.fori_loop(1, n - 1, one, 0)
-    for part, (start, size) in enumerate(pieces):
+    for part, (which, way, start, _, size) in enumerate(pieces):
+        slot = slot_of(n - 2, part)
+        copy_of(n - 2, part, slot).wait_recv()
         columns = pl.ds(start, size)
-        copy_of(n - 2, part, held.at[n - 2, :, columns]).wait_recv()
-        o_ref[:, columns] = held[n - 2, :, columns].astype(jnp.float32) + g_ref[
+        o_refs[which][:, columns] = slot[...].astype(jnp.float32) + g_refs[which][
             me, :, columns
         ].astype(jnp.float32)
 
     def drain(step, carry):
-        for part, (start, size) in enumerate(pieces):
-            copy_of(step, part, held.at[step, :, pl.ds(start, size)]).wait_send()
+        for part in range(len(pieces)):
+            copy_of(step, part, slot_of(step, part)).wait_send()
         return carry
 
     lax.fori_loop(0, n - 1, drain, 0)
 
 
-def ring_sum(g, axis, ident):
-    n, rows, columns = g.shape
+def ring_sum(gs, plan, axis, ident):
+    n, rows, _ = gs[0].shape
+    pieces, at = [], 0
+    for which, way, start, size in plan:
+        pieces.append((which, way, start, at, size))
+        at += size
     return pl.pallas_call(
-        functools.partial(ring_sum_kernel, n, axis),
+        functools.partial(ring_sum_kernel, n, axis, tuple(pieces), len(gs)),
+        out_shape=tuple(jax.ShapeDtypeStruct(g.shape[1:], jnp.float32) for g in gs),
+        in_specs=[pl.BlockSpec(memory_space=pltpu.VMEM)] * len(gs),
+        out_specs=tuple(pl.BlockSpec(memory_space=pltpu.VMEM) for _ in gs),
+        scratch_shapes=[
+            pltpu.VMEM((n - 1, rows, at), gs[0].dtype),
+            pltpu.SemaphoreType.DMA((n - 1, len(pieces))),
+            pltpu.SemaphoreType.DMA((n - 1, len(pieces))),
+        ],
+        compiler_params=pltpu.CompilerParams(collective_id=ident, has_side_effects=True),
+    )(*gs)
+
+
+def scatter_sum_kernel(axis, x_ref, o_ref, near, far, total, send_sem, recv_sem):
+    me, beside, across = quad(axis)
+    greet((axis, beside), (axis, across))
+    half = o_ref.shape[0] // 2
+    parts = [pl.ds(0, half), pl.ds(half, half)]
+
+    def pair(i, k, chunk):
+        return remote(
+            x_ref.at[chunk, parts[i]],
+            near.at[k, parts[i]],
+            send_sem.at[i, k],
+            recv_sem.at[i, k],
+            axis,
+            beside,
+        )
+
+    copies = [pair(i, 0, (beside + 2) % 4) for i in range(2)]
+    copies += [pair(i, 1, beside) for i in range(2)]
+    for copy in copies:
+        copy.start()
+    crossing = []
+    for i, rows in enumerate(parts):
+        copies[i].wait_recv()
+        total[rows] = (
+            x_ref[across, rows].astype(jnp.float32) + near[0, rows].astype(jnp.float32)
+        ).astype(total.dtype)
+        copy = remote(
+            total.at[rows], far.at[rows], send_sem.at[i, 2], recv_sem.at[i, 2], axis, across
+        )
+        copy.start()
+        crossing.append(copy)
+    for i, rows in enumerate(parts):
+        copies[2 + i].wait_recv()
+        crossing[i].wait_recv()
+        o_ref[rows] = (
+            x_ref[me, rows].astype(jnp.float32)
+            + near[1, rows].astype(jnp.float32)
+            + far[rows].astype(jnp.float32)
+        )
+    for copy in copies + crossing:
+        copy.wait_send()
+
+
+def scatter_sum(x, axis, ident):
+    rows, columns = x.shape[0] // 4, x.shape[1]
+    return pl.pallas_call(
+        functools.partial(scatter_sum_kernel, axis),
         out_shape=jax.ShapeDtypeStruct((rows, columns), jnp.float32),
         in_specs=[pl.BlockSpec(memory_space=pltpu.VMEM)],
         out_specs=pl.BlockSpec(memory_space=pltpu.VMEM),
         scratch_shapes=[
-            pltpu.VMEM((n - 1, rows, columns), g.dtype),
-            pltpu.SemaphoreType.DMA((n - 1, 4)),
-            pltpu.SemaphoreType.DMA((n - 1, 4)),
+            pltpu.VMEM((2, rows, columns), x.dtype),
+            pltpu.VMEM((rows, columns), x.dtype),
+            pltpu.VMEM((rows, columns), x.dtype),
+            pltpu.SemaphoreType.DMA((2, 3)),
+            pltpu.SemaphoreType.DMA((2, 3)),
         ],
         compiler_params=pltpu.CompilerParams(collective_id=ident, has_side_effects=True),
-    )(g)
-
-
-def gather_kernel(n, axis, x_ref, o_ref, send_sem, recv_sem):
-    me = lax.axis_index(axis)
-    peers = [(me + k) % n for k in range(1, n)]
-    greet(axis, peers)
-    copies = []
-    for k, peer in enumerate(peers):
-        copy = pltpu.make_async_remote_copy(
-            src_ref=x_ref,
-            dst_ref=o_ref.at[me],
-            send_sem=send_sem.at[k],
-            recv_sem=recv_sem.at[k],
-            device_id={axis: peer},
-            device_id_type=MESH,
-        )
-        copy.start()
-        copies.append(copy)
-    o_ref[me] = x_ref[...]
-    for copy in copies:
-        copy.wait()
-
-
-def gather(x, axis, ident):
-    n = lax.axis_size(axis)
-    return pl.pallas_call(
-        functools.partial(gather_kernel, n, axis),
-        out_shape=jax.ShapeDtypeStruct((n,) + x.shape, x.dtype),
-        in_specs=[pl.BlockSpec(memory_space=pltpu.VMEM)],
-        out_specs=pl.BlockSpec(memory_space=pltpu.VMEM),
-        scratch_shapes=[
-            pltpu.SemaphoreType.DMA((n - 1,)),
-            pltpu.SemaphoreType.DMA((n - 1,)),
-        ],
-        compiler_params=pltpu.CompilerParams(collective_id=ident, has_side_effects=True),
-    )(x)
-
-
-def scatter_sum_kernel(n, axis, x_ref, o_ref, held, send_sem, recv_sem):
-    me = lax.axis_index(axis)
-    peers = [(me + k) % n for k in range(1, n)]
-    greet(axis, peers)
-    copies = []
-    for k, peer in enumerate(peers):
-        copy = pltpu.make_async_remote_copy(
-            src_ref=x_ref.at[peer],
-            dst_ref=held.at[k],
-            send_sem=send_sem.at[k],
-            recv_sem=recv_sem.at[k],
-            device_id={axis: peer},
-            device_id_type=MESH,
-        )
-        copy.start()
-        copies.append(copy)
-    for copy in copies:
-        copy.wait()
-    total = x_ref[me].astype(jnp.float32)
-    for k in range(n - 1):
-        total = total + held[k].astype(jnp.float32)
-    o_ref[...] = total
-
-
-def scatter_sum(x, axis, ident):
-    n = lax.axis_size(axis)
-    rows, columns = x.shape[0] // n, x.shape[1]
-    return pl.pallas_call(
-        functools.partial(scatter_sum_kernel, n, axis),
-        out_shape=jax.ShapeDtypeStruct((rows, columns), jnp.float32),
-        in_specs=[pl.BlockSpec(memory_space=pltpu.VMEM)],
-        out_specs=pl.BlockSpec(memory_space=pltpu.VMEM),
-        scratch_shapes=[
-            pltpu.VMEM((n - 1, rows, columns), x.dtype),
-            pltpu.SemaphoreType.DMA((n - 1,)),
-            pltpu.SemaphoreType.DMA((n - 1,)),
-        ],
-        compiler_params=pltpu.CompilerParams(collective_id=ident, has_side_effects=True),
-    )(x.reshape(n, rows, columns))
+    )(x.reshape(4, rows, columns))
 
 
 def chain(decay, state, first, last, backward, ident):
@@ -252,7 +371,7 @@
     lines = jnp.zeros((16, DV), jnp.float32)
     lines = lines.at[0, :DK].set(decay).at[1, 0].set(first).at[1, 1].set(last)
     block = jnp.concatenate([state, lines], axis=0).astype(jnp.bfloat16)
-    every = gather(block, "shard", ident)
+    every = ring_gather(block, "shard", ident)
     states = every[:, :DK].astype(jnp.float32)
     decays = every[:, DK, :DK].astype(jnp.float32)
     firsts = every[:, DK + 1, 0].astype(jnp.float32)
@@ -374,7 +493,10 @@
     )
     used = packed.shape[1]
     packed = jnp.pad(packed, ((0, 0), (0, -used % LANE)))
-    every = ring_gather(packed, "shard", 1)
+    inv_attn = rms_scale(resid_in)
+    unit_rows = (resid_in * inv_attn).astype(jnp.bfloat16)
+    cot_rows = cotangent.astype(jnp.bfloat16)
+    every, both = enter(packed, jnp.concatenate([unit_rows, cot_rows], axis=1), 1)
     spread = every.reshape(n * rows, packed.shape[1])
     edge_out = 2 * DK + 2 * DV
     edge_gate = edge_out + DV
@@ -394,11 +516,9 @@
     length = segment.shape[0]
     local_heads = 1
     scale = DK ** (-0.5)
-    inv_attn = rms_scale(resid_in)
-    normed_rows = (resid_in * inv_attn * gain_attn).astype(jnp.bfloat16)
-    cot_rows = cotangent.astype(jnp.bfloat16)
-    both = gather(jnp.concatenate([normed_rows, cot_rows], axis=1), "head", 2)
-    normed_in = both[:, :, :D].reshape(length, D)
+    normed_in = (
+        (both[:, :, :D].astype(jnp.float32) * gain_attn).astype(jnp.bfloat16).reshape(length, D)
+    )
     cot_bf = both[:, :, D:].reshape(length, D)
     projected = jnp.dot(normed_in, project_w, preferred_element_type=jnp.float32)
     query = projected[:, :DK].reshape(length, local_heads, DK)
@@ -541,31 +661,41 @@
         a = a.reshape(n, a.shape[0] // n, -1)
         return jnp.pad(a, ((0, 0), (0, rows - a.shape[1]), (0, 0))).reshape(D, -1)
 
-    grads = jnp.concatenate(
+    lean = jnp.concatenate(
         [
-            g.astype(jnp.bfloat16)
-            for g in (
-                grad_project,
-                grad_out,
-                grad_gu,
-                grad_down,
-                part_low,
-                part_attn_gain[:, None],
-                part_mlp_gain[:, None],
-                owners(part_head_gain),
-                owners(grad_rank[:, 0, :].T),
-                owners(grad_bias[0]),
-            )
+            part_low,
+            part_attn_gain[:, None],
+            part_mlp_gain[:, None],
+            owners(part_head_gain),
+            owners(grad_rank[:, 0, :].T),
+            owners(grad_bias[0]),
         ],
         axis=1,
     )
-    grads = jnp.pad(grads, ((0, 0), (0, packed.shape[1] - used)))
-    owned = ring_sum(grads.reshape(n, rows, packed.shape[1]), "shard", 10)
+    lean = jnp.pad(lean, ((0, 0), (0, packed.shape[1] - used)))
+    grads = [
+        g.astype(jnp.bfloat16).reshape(n, rows, -1)
+        for g in (
+            grad_project,
+            grad_out,
+            grad_gu,
+            jnp.concatenate([grad_down, lean], axis=1),
+        )
+    ]
+    middle = (wide // LANE + 1) * LANE
+    plan = (
+        (2, 0, 0, middle),
+        (3, 1, 0, grads[3].shape[2]),
+        (0, 0, 0, edge_out),
+        (2, 1, middle, 2 * wide - middle),
+        (1, 1, 0, DV),
+    )
+    own_project, own_out, own_gu, own_rest = ring_sum(grads, plan, "shard", 10)
     heads = lax.axis_size("head")
-    shared = owned[:, edge_low : edge_low + GATE_RANK + 3]
+    shared = own_rest[:, wide : wide + GATE_RANK + 3]
     gain_rows = DV // n
-    final_rank = owned[: DK // n, edge_low + GATE_RANK + 3 : edge_low + 2 * GATE_RANK + 3]
-    final_bias = owned[: DK // n, edge_low + 2 * GATE_RANK + 3]
+    final_rank = own_rest[: DK // n, wide + GATE_RANK + 3 : wide + 2 * GATE_RANK + 3]
+    final_bias = own_rest[: DK // n, wide + 2 * GATE_RANK + 3]
     shares = jnp.concatenate(
         [
             shared[:, : GATE_RANK + 2].reshape(heads, rows // heads, GATE_RANK + 2),
@@ -576,7 +706,7 @@
         ],
         axis=2,
     )
-    deep = max(rows // heads, 16)
+    deep = max(rows // heads, 32)
     shares = jnp.pad(
         shares, ((0, 0), (0, deep - rows // heads), (0, LANE - GATE_RANK - 3))
     ).reshape(heads * deep, LANE)
@@ -585,19 +715,19 @@
         resid_out,
         grad_in,
         final[:, GATE_RANK],
-        owned[:, :DK],
-        owned[:, DK : 2 * DK],
-        owned[:, 2 * DK : 2 * DK + DV],
-        owned[:, 2 * DK + DV : edge_out],
+        own_project[:, :DK],
+        own_project[:, DK : 2 * DK],
+        own_project[:, 2 * DK : 2 * DK + DV],
+        own_project[:, 2 * DK + DV :],
         final[:, :GATE_RANK],
         final_rank.T.reshape(GATE_RANK, 1, DK // n),
         final_bias.reshape(1, DK // n),
         final[: gain_rows // heads, GATE_RANK + 2],
-        owned[:, edge_out:edge_gate].T,
+        own_out.T,
         final[:, GATE_RANK + 1],
-        owned[:, edge_gate : edge_gate + wide],
-        owned[:, edge_gate + wide : edge_down],
-        owned[:, edge_down:edge_low].T,
+        own_gu[:, :wide],
+        own_gu[:, wide:],
+        own_rest[:, :wide].T,
     )
 
 

time: 417 us -> 360 us (0.86)
  local copies, waits for them, and re-layouts: 62.7 us -> 29.4 us
  Pallas kernels: 254 us -> 226 us
  matrix products: 43.8 us -> 51.2 us
    pallas_call x1 -> x2, Pallas kernels: 69.5 us -> 33.4 us  [ring_gather(): pl.pallas_call(functools.partial(ring_gather_kernel, n, axis), out_shape=...]
    concatenate x1, local copies, waits for them, and re-layouts: 10.7 us -> 0.48 us  [on_device(): jnp.concatenate([part_low, part_attn_gain[:, None], part_mlp_gain[:, None...]
    pallas_call x10 -> x8, Pallas kernels: 184 us -> 193 us  [the longest x1 71.5 us: ring_sum(): pl.pallas_call(functools.partial(ring_sum_kernel, n, axis, tuple(pieces),...]
    convert_element_type x6 -> x0, local copies, waits for them, and re-layouts: 7.89 us -> none  [on_device(): g.astype(jnp.bfloat16)]
    pad x1, local copies, waits for them, and re-layouts: 6.01 us -> 0.06 us  [on_device(): lean = jnp.pad(lean, ((0, 0), (0, packed.shape[1] - used)))]
    dot_general x11, matrix products: 3.3 us -> 9.08 us  [advance(): jnp.einsum('zie,zir->ier', key_final_rows, value_segment, precision=HIGH_...]
    unnamed x188 -> x174, local copies, waits for them, and re-layouts: 13.2 us -> 11.3 us
where the time goes in v2:
time: 360 us; the launch traced here: 357 us
  Pallas kernels  226 us (63%)
  matrix products  51.2 us (14%)
  other arithmetic  40.5 us (11%)
  local copies, waits for them, and re-layouts  29.4 us (8%)
  between operations  10.2 us (3%)
    pallas_call x1, Pallas kernels, ring_sum(): pl.pallas_call(functools.partial(ring_sum_kernel, n, axis, tuple(pieces),...  71.5 us
    pallas_call x1, Pallas kernels, enter(): pl.pallas_call(functools.partial(enter_kernel, n), out_shape=(jax.ShapeDt...  70.6 us
    pallas_call x4, Pallas kernels, scatter_sum(): pl.pallas_call(functools.partial(scatter_sum_kernel, axis), out_shape=jax...  34.4 us
    pallas_call x2, Pallas kernels, ring_gather(): pl.pallas_call(functools.partial(ring_gather_kernel, n, axis), out_shape=...  33.4 us
    pallas_call x2, Pallas kernels, gather(): pl.pallas_call(functools.partial(gather_kernel, axis), out_shape=jax.Shap...  16.2 us
    unnamed x174, local copies, waits for them, and re-layouts  11.3 us
    dot_general x11, matrix products, advance(): jnp.einsum('zie,zir->ier', key_final_rows, value_segment, precision=HIGH_...  9.08 us

profile of v2, /device:TPU:0, one launch (start us, length us, event | category | flops | bytes accessed | tf_op | source)
XLA Modules:
  0.0 357.4 jit_solution(10375312332428288813)
XLA Ops:
  12.7 70.6 %shard_map.288 = (bf16[8,128,3200]{2,1,0:T(8,128)(2,1)}, bf16[4,64,2048]{2,1,0:T(8,128)(2,1)}) custom-call(bf16[128,3200]{1,0:T(8,128)(2,1)} %pad.87.w_ref, bf16[64,2048]{1,0:T(8,128)(2,1)} %pad_maximum_fusion.6.x_ref), custom_call_target="tpu_custom_call" | custom-call | tf_op jit(solution)/shard_map/pallas_call | solution.py:208
  90.4 2.0 fusion.10
  97.8 17.1 %shard_map.289 = bf16[8,144,256]{2,1,0:T(8,128)(2,1)} custom-call(bf16[144,256]{1,0:T(8,128)(2,1)} %pad_maximum_fusion.10.x_ref), custom_call_target="tpu_custom_call" | custom-call | tf_op jit(solution)/shard_map/pallas_call | solution.py:114
  120.2 3.8 %compare_convert_fusion = (f32[64]{0:T(128)}, f32[64]{0:T(128)S(1)}, f32[64]{0:T(128)S(1)}, f32[64]{0:T(128)S(1)}, f32[64]{0:T(128)S(1)}, /*index=5*/f32[64]{0:T(128)S(1)}, f32[64]{0:T(128)S(1)}, f32[64]{0:T(128)S(1)}) fusion(f32[]{:T(128)} %bitcast.26, f32[256]{0:T(256)S(1)} %convert_add_fusion, f32[]{:T(128)} %fusion.202, f32[]{:T(128)} %bitcast.40, ...), kind=kLoop, calls=%fused_computation.355 | loop fusion | flops 1024 | bytes 3092 | tf_op jit(solution)/shard_map/jvp()/eval_jaxpr/convert_element_type | solution.py:428
  134.5 2.2 convolution_convert_fusion.4
  136.8 8.9 %shard_map.290 = f32[64,1024]{1,0:T(8,128)} custom-call(bf16[4,64,1024]{2,1,0:T(8,128)(2,1)} %bitcast.702), custom_call_target="tpu_custom_call" | custom-call | tf_op jit(solution)/shard_map/pallas_call | solution.py:352
  148.0 8.2 %shard_map.291 = bf16[4,64,1024]{2,1,0:T(8,128)(2,1)} custom-call(bf16[64,1024]{1,0:T(8,128)(2,1)} %multiply_convert_fusion.5.x_ref), custom_call_target="tpu_custom_call" | custom-call | tf_op jit(solution)/shard_map/pallas_call | solution.py:183
  156.2 3.1 fusion.2
  159.4 2.3 multiply_convert_fusion.2
  164.7 12.1 %shard_map.292 = f32[64,2048]{1,0:T(8,128)} custom-call(bf16[4,64,2048]{2,1,0:T(8,128)(2,1)} %bitcast.692), custom_call_target="tpu_custom_call" | custom-call | tf_op jit(solution)/shard_map/pallas_call | solution.py:352
  176.8 1.6 multiply_reduce_fusion.2
  178.4 2.0 fusion.222
  180.4 8.0 %shard_map.293 = bf16[4,64,1024]{2,1,0:T(8,128)(2,1)} custom-call(bf16[64,1024]{1,0:T(8,128)(2,1)} %get-tuple-element.186.x_ref), custom_call_target="tpu_custom_call" | custom-call | tf_op jit(solution)/shard_map/pallas_call | solution.py:183
  188.4 2.8 fusion.71
  196.2 16.3 %shard_map.294 = bf16[8,144,256]{2,1,0:T(8,128)(2,1)} custom-call(bf16[144,256]{1,0:T(8,128)(2,1)} %pad_maximum_fusion.11.x_ref), custom_call_target="tpu_custom_call" | custom-call | tf_op jit(solution)/shard_map/pallas_call | solution.py:114
  242.3 3.0 fusion.15
  245.3 8.0 %shard_map.295 = f32[64,1024]{1,0:T(8,128)} custom-call(bf16[4,64,1024]{2,1,0:T(8,128)(2,1)} %bitcast.708), custom_call_target="tpu_custom_call" | custom-call | tf_op jit(solution)/shard_map/pallas_call | solution.py:352
  253.3 1.7 multiply_reduce_fusion.3
  256.2 1.7 convolution_convert_fusion.2
  257.9 1.7 copy.233
  261.1 2.6 convolution_convert_fusion
  264.9 1.8 convolution_convert_fusion.1
  266.7 71.5 %shard_map.296 = (f32[128,768]{1,0:T(8,128)}, f32[128,256]{1,0:T(8,128)}, f32[128,1408]{1,0:T(8,128)}, f32[128,768]{1,0:T(8,128)}) custom-call(bf16[8,128,768]{2,1,0:T(8,128)(2,1)} %bitcast.704, bf16[8,128,256]{2,1,0:T(8,128)(2,1)} %bitcast.697, bf16[8,128,1408]{2,1,0:T(8,128)(2,1)} %bitcast.634, bf16[8,128,768]{2,1,0:T(8,128)(2,1)} %pad_maximum_fusion.refs_3_), custom_call_target="tpu_custom_call" | custom-call | tf_op jit(solution)/shard_map/pallas_call | solution.py:293
  343.3 5.4 %shard_map.297 = f32[32,128]{1,0:T(8,128)} custom-call(bf16[4,32,128]{2,1,0:T(8,128)(2,1)} %pad.97.x_ref), custom_call_target="tpu_custom_call" | custom-call | tf_op jit(solution)/shard_map/pallas_call | solution.py:352
  (362 shorter events, 88.7 us)
Async XLA Ops:
  124.0 12.7 %copy-start.53 = (f32[64]{0:T(128)}, f32[64]{0:T(128)S(1)}, u32[]{:S(2)}) copy-start(f32[64]{0:T(128)S(1)} %get-tuple-element.226) | copy-start | bytes 772
  124.0 12.7 %copy-start.54 = (f32[64]{0:T(128)}, f32[64]{0:T(128)S(1)}, u32[]{:S(2)}) copy-start(f32[64]{0:T(128)S(1)} %get-tuple-element.224) | copy-start | bytes 772
  124.2 12.5 %copy-start.43 = (f32[64]{0:T(128)}, f32[64]{0:T(128)S(1)}, u32[]{:S(2)}) copy-start(f32[64]{0:T(128)S(1)} %get-tuple-element.228) | copy-start | bytes 772
  127.1 18.5 %copy-start = (f32[64,1024]{1,0:T(8,128)S(1)}, f32[64,1024]{1,0:T(8,128)}, u32[]{:S(2)}) copy-start(f32[64,1024]{1,0:T(8,128)} %param.29) | copy-start | bytes 786436
  147.3 12.1 %copy-start.64 = (f32[64]{0:T(128)}, f32[64]{0:T(128)S(1)}, u32[]{:S(2)}) copy-start(f32[64]{0:T(128)S(1)} %get-tuple-element.239) | copy-start | bytes 772
  163.6 14.8 %copy-start.9 = (f32[64,1024]{1,0:T(8,128)S(1)}, f32[64,1024]{1,0:T(8,128)}, u32[]{:S(2)}) copy-start(f32[64,1024]{1,0:T(8,128)} %param.30) | copy-start | bytes 786436
  191.2 33.3 %copy-start.42 = (f32[64]{0:T(128)S(1)}, f32[64]{0:T(128)}, u32[]{:S(2)}) copy-start(f32[64]{0:T(128)} %copy-done.41) | copy-start | bytes 772
  192.1 32.9 %copy-start.50 = (f32[64]{0:T(128)S(1)}, f32[64]{0:T(128)}, u32[]{:S(2)}) copy-start(f32[64]{0:T(128)} %copy-done.49) | copy-start | bytes 772
  217.4 13.8 %copy-start.52 = (f32[64]{0:T(128)S(1)}, f32[64]{0:T(128)}, u32[]{:S(2)}) copy-start(f32[64]{0:T(128)} %copy-done.51) | copy-start | bytes 772
  218.4 13.3 %copy-start.59 = (f32[128]{0:T(128)S(1)}, f32[128]{0:T(128)}, u32[]{:S(2)}) copy-start(f32[128]{0:T(128)} %copy-done.58) | copy-start | bytes 1540
  220.6 13.2 %copy-start.26 = (f32[256,128]{1,0:T(8,128)S(1)}, f32[256,128]{1,0:T(8,128)}, u32[]{:S(2)}) copy-start(f32[256,128]{1,0:T(8,128)} %get-tuple-element.241) | copy-start | bytes 393220
  221.7 12.2 %copy-start.34 = (f32[256,16]{0,1:T(8,128)S(1)}, f32[256,16]{0,1:T(8,128)}, u32[]{:S(2)}) copy-start(f32[256,16]{0,1:T(8,128)} %copy-done.33) | copy-start | bytes 49156
  228.9 11.5 %copy-start.22 = (f32[64,64]{1,0:T(8,128)S(1)}, f32[64,64]{1,0:T(8,128)}, u32[]{:S(2)}) copy-start(f32[64,64]{1,0:T(8,128)} %copy-done.21) | copy-start | bytes 49156
  230.0 11.6 %copy-start.24 = (f32[64,64]{1,0:T(8,128)S(1)}, f32[64,64]{1,0:T(8,128)}, u32[]{:S(2)}) copy-start(f32[64,64]{1,0:T(8,128)} %copy-done.23) | copy-start | bytes 49156
  242.2 12.9 %copy-start.73 = (bf16[256]{0:T(256)(128)(2,1)S(1)}, bf16[256]{0:T(256)(128)(2,1)}, u32[]{:S(2)}) copy-start(bf16[256]{0:T(256)(128)(2,1)} %get-tuple-element.166) | copy-start | bytes 1540
  242.2 13.0 %copy-start.56 = (bf16[1024]{0:T(1024)(128)(2,1)S(1)}, bf16[1024]{0:T(1024)(128)(2,1)}, u32[]{:S(2)}) copy-start(bf16[1024]{0:T(1024)(128)(2,1)} %get-tuple-element.168) | copy-start | bytes 6148
  242.3 13.7 %copy-start.5 = (bf16[4,64,1024]{2,1,0:T(8,128)(2,1)S(1)}, bf16[4,64,1024]{2,1,0:T(8,128)(2,1)}, u32[]{:S(2)}) copy-start(bf16[4,64,1024]{2,1,0:T(8,128)(2,1)} %copy-done.4) | copy-start | bytes 1572868
  242.3 13.9 %copy-start.15 = (bf16[256,704]{1,0:T(8,128)(2,1)S(1)}, bf16[256,704]{1,0:T(8,128)(2,1)}, u32[]{:S(2)}) copy-start(bf16[256,704]{1,0:T(8,128)(2,1)} %copy-done.14) | copy-start | bytes 1081348
  338.3 14.7 %copy-start.16 = (f32[128,768]{1,0:T(8,128)S(1)}, f32[128,768]{1,0:T(8,128)}, u32[]{:S(2)}) copy-start(f32[128,768]{1,0:T(8,128)} %get-tuple-element.97) | copy-start | bytes 1179652
  338.3 16.1 %copy-start.29 = (f32[128,256]{1,0:T(8,128)S(1)}, f32[128,256]{1,0:T(8,128)}, u32[]{:S(2)}) copy-start(f32[128,256]{1,0:T(8,128)} %get-tuple-element.98) | copy-start | bytes 393220
  339.7 16.9 %copy-start.74 = (f32[64]{0:T(128)S(1)}, f32[64]{0:T(128)}, u32[]{:S(2)}) copy-start(f32[64]{0:T(128)} %get-tuple-element.173) | copy-start | bytes 772
  339.7 16.9 %copy-start.2 = (f32[64,1024]{1,0:T(8,128)S(1)}, f32[64,1024]{1,0:T(8,128)}, u32[]{:S(2)}) copy-start(f32[64,1024]{1,0:T(8,128)} %shard_map.295) | copy-start | bytes 786436
  339.7 16.9 %copy-start.8 = (f32[64,1024]{1,0:T(8,128)S(1)}, f32[64,1024]{1,0:T(8,128)}, u32[]{:S(2)}) copy-start(f32[64,1024]{1,0:T(8,128)} %get-tuple-element.187) | copy-start | bytes 786436
  339.7 16.9 %copy-start.71 = (f32[64]{0:T(128)S(1)}, f32[64]{0:T(128)}, u32[]{:S(2)}) copy-start(f32[64]{0:T(128)} %get-tuple-element.236) | copy-start | bytes 772
  (54 other events, 286.3 us)

commit v3 on v2

--- a/solution.py
+++ b/solution.py
@@ -468,10 +468,16 @@
     wide = w_gate.shape[1]
     rows = w_query.shape[0]
 
-    def tall(a):
-        a = a.reshape(a.shape[0], -1)
-        return jnp.pad(a, ((0, rows - a.shape[0]), (0, 0)))
-
+    def line(a):
+        return jnp.pad(a, (0, LANE - a.shape[0]))[None]
+
+    def filled(a, height, width):
+        return jnp.pad(a, ((0, height - a.shape[0]), (0, width - a.shape[1])))
+
+    spare = -(3 * wide + GATE_RANK) % LANE
+    lines = jnp.concatenate(
+        [line(attn_gain), line(mlp_gain), line(head_gain), line(rank_bias[0])], axis=0
+    )
     packed = jnp.concatenate(
         [
             w_query,
@@ -483,20 +489,14 @@
             w_up,
             w_down.T,
             w_low,
-            tall(attn_gain),
-            tall(mlp_gain),
-            tall(head_gain),
-            tall(w_rank[:, 0, :].T),
-            tall(rank_bias[0]),
+            filled(w_rank[:, 0, :], rows, spare),
+            filled(lines, rows, LANE),
         ],
         axis=1,
     )
-    used = packed.shape[1]
-    packed = jnp.pad(packed, ((0, 0), (0, -used % LANE)))
     inv_attn = rms_scale(resid_in)
-    unit_rows = (resid_in * inv_attn).astype(jnp.bfloat16)
-    cot_rows = cotangent.astype(jnp.bfloat16)
-    every, both = enter(packed, jnp.concatenate([unit_rows, cot_rows], axis=1), 1)
+    unit_rows = resid_in * inv_attn
+    every, both = enter(packed, jnp.concatenate([unit_rows, cotangent], axis=1), 1)
     spread = every.reshape(n * rows, packed.shape[1])
     edge_out = 2 * DK + 2 * DV
     edge_gate = edge_out + DV
@@ -506,20 +506,25 @@
     out_wt = spread[:, edge_out:edge_gate]
     gu_w = spread[:, edge_gate:edge_down]
     down_wt = spread[:, edge_down:edge_low]
-    tail = every[:, :, edge_low:]
+    tail = every[:, :, edge_low : edge_low + GATE_RANK + spare]
+    vectors = every[:, :4, edge_low + GATE_RANK + spare :]
     low_w = tail[:, :, :GATE_RANK].reshape(D, GATE_RANK)
-    gain_attn = tail[:, :, GATE_RANK].reshape(D).astype(jnp.float32)
-    gain_mlp = tail[:, :, GATE_RANK + 1].reshape(D).astype(jnp.float32)
-    gain_head = tail[:, : DV // n, GATE_RANK + 2].reshape(DV).astype(jnp.float32)
-    rank_w = tail[:, : DK // n, GATE_RANK + 3 : 2 * GATE_RANK + 3].reshape(DK, GATE_RANK).T
-    bias_w = tail[:, : DK // n, 2 * GATE_RANK + 3].reshape(DK)
+    gain_attn = vectors[:, 0, :rows].reshape(D).astype(jnp.float32)
+    gain_mlp = vectors[:, 1, :rows].reshape(D).astype(jnp.float32)
+    gain_head = vectors[:, 2, : DV // n].reshape(DV).astype(jnp.float32)
+    bias_w = vectors[:, 3, : DK // n].reshape(DK)
+    rank_w = (
+        tail[:, :GATE_RANK, GATE_RANK : GATE_RANK + DK // n]
+        .transpose(1, 0, 2)
+        .reshape(GATE_RANK, DK)
+    )
     length = segment.shape[0]
     local_heads = 1
     scale = DK ** (-0.5)
     normed_in = (
-        (both[:, :, :D].astype(jnp.float32) * gain_attn).astype(jnp.bfloat16).reshape(length, D)
-    )
-    cot_bf = both[:, :, D:].reshape(length, D)
+        (both[:, :, :D] * gain_attn).astype(jnp.bfloat16).reshape(length, D)
+    )
+    cot_bf = both[:, :, D:].reshape(length, D).astype(jnp.bfloat16)
     projected = jnp.dot(normed_in, project_w, preferred_element_type=jnp.float32)
     query = projected[:, :DK].reshape(length, local_heads, DK)
     key = projected[:, DK : 2 * DK].reshape(length, local_heads, DK)
@@ -657,32 +662,39 @@
         - resid_in * inv_attn**3 * jnp.mean(scaled_in * resid_in, axis=-1, keepdims=True)
     )
 
-    def owners(a):
-        a = a.reshape(n, a.shape[0] // n, -1)
-        return jnp.pad(a, ((0, 0), (0, rows - a.shape[1]), (0, 0))).reshape(D, -1)
-
-    lean = jnp.concatenate(
-        [
-            part_low,
-            part_attn_gain[:, None],
-            part_mlp_gain[:, None],
-            owners(part_head_gain),
-            owners(grad_rank[:, 0, :].T),
-            owners(grad_bias[0]),
-        ],
+    def block(a):
+        a = a.reshape(n, 1, -1)
+        return jnp.pad(a, ((0, 0), (0, 0), (0, LANE - a.shape[2])))
+
+    ranks = grad_rank[:, 0, :].reshape(GATE_RANK, n, DK // n).transpose(1, 0, 2)
+    ranks = jnp.pad(
+        ranks, ((0, 0), (0, rows - GATE_RANK), (0, spare - DK // n))
+    ).astype(jnp.bfloat16)
+    sums = jnp.concatenate(
+        [block(part_attn_gain), block(part_mlp_gain), block(part_head_gain), block(grad_bias)],
         axis=1,
     )
-    lean = jnp.pad(lean, ((0, 0), (0, packed.shape[1] - used)))
+    sums = jnp.pad(sums, ((0, 0), (0, rows - 4), (0, 0))).astype(jnp.bfloat16)
     grads = [
         g.astype(jnp.bfloat16).reshape(n, rows, -1)
         for g in (
             grad_project,
             grad_out,
             grad_gu,
-            jnp.concatenate([grad_down, lean], axis=1),
         )
     ]
-    middle = (wide // LANE + 1) * LANE
+    grads.append(
+        jnp.concatenate(
+            [
+                grad_down.astype(jnp.bfloat16).reshape(n, rows, wide),
+                part_low.astype(jnp.bfloat16).reshape(n, rows, GATE_RANK),
+                ranks,
+                sums,
+            ],
+            axis=2,
+        )
+    )
+    middle = (wide // LANE + 2) * LANE
     plan = (
         (2, 0, 0, middle),
         (3, 1, 0, grads[3].shape[2]),
@@ -692,39 +704,37 @@
     )
     own_project, own_out, own_gu, own_rest = ring_sum(grads, plan, "shard", 10)
     heads = lax.axis_size("head")
-    shared = own_rest[:, wide : wide + GATE_RANK + 3]
     gain_rows = DV // n
-    final_rank = own_rest[: DK // n, wide + GATE_RANK + 3 : wide + 2 * GATE_RANK + 3]
-    final_bias = own_rest[: DK // n, wide + 2 * GATE_RANK + 3]
-    shares = jnp.concatenate(
-        [
-            shared[:, : GATE_RANK + 2].reshape(heads, rows // heads, GATE_RANK + 2),
-            jnp.pad(
-                shared[:gain_rows, GATE_RANK + 2].reshape(heads, gain_rows // heads, 1),
-                ((0, 0), (0, (rows - gain_rows) // heads), (0, 0)),
-            ),
-        ],
-        axis=2,
-    )
-    deep = max(rows // heads, 32)
-    shares = jnp.pad(
-        shares, ((0, 0), (0, deep - rows // heads), (0, LANE - GATE_RANK - 3))
-    ).reshape(heads * deep, LANE)
-    final = scatter_sum(shares.astype(jnp.bfloat16), "head", 11)[: rows // heads]
+    edge_lines = wide + GATE_RANK + spare
+    final_rank = own_rest[:GATE_RANK, wide + GATE_RANK : wide + GATE_RANK + DK // n]
+    final_bias = own_rest[3, edge_lines : edge_lines + DK // n]
+
+    def owned_by(row, size):
+        a = own_rest[row, edge_lines : edge_lines + size].reshape(heads, 1, size // heads)
+        return jnp.pad(a, ((0, 0), (0, 0), (0, LANE - size // heads)))
+
+    shares = jnp.concatenate([owned_by(0, rows), owned_by(1, rows), owned_by(2, gain_rows)], axis=1)
+    low_share = own_rest[:, wide : wide + GATE_RANK].reshape(heads, rows // heads, GATE_RANK)
+    low_share = jnp.pad(low_share, ((0, 0), (0, 0), (0, LANE - GATE_RANK)))
+    shares = jnp.concatenate([low_share, shares], axis=1)
+    deep = -(-(rows // heads + 3) // 32) * 32
+    shares = jnp.pad(shares, ((0, 0), (0, deep - shares.shape[1]), (0, 0)))
+    final = scatter_sum(shares.reshape(heads * deep, LANE).astype(jnp.bfloat16), "head", 11)
+    low_rows = rows // heads
     return (
         resid_out,
         grad_in,
-        final[:, GATE_RANK],
+        final[low_rows, :low_rows],
         own_project[:, :DK],
         own_project[:, DK : 2 * DK],
         own_project[:, 2 * DK : 2 * DK + DV],
         own_project[:, 2 * DK + DV :],
-        final[:, :GATE_RANK],
-        final_rank.T.reshape(GATE_RANK, 1, DK // n),
+        final[:low_rows, :GATE_RANK],
+        final_rank.reshape(GATE_RANK, 1, DK // n),
         final_bias.reshape(1, DK // n),
-        final[: gain_rows // heads, GATE_RANK + 2],
+        final[low_rows + 2, : gain_rows // heads],
         own_out.T,
-        final[:, GATE_RANK + 1],
+        final[low_rows + 1, :low_rows],
         own_gu[:, :wide],
         own_gu[:, wide:],
         own_rest[:, :wide].T,

time: 360 us -> 360 us (level)
    unnamed x174 -> x168, local copies, waits for them, and re-layouts: 11.3 us -> 9.1 us
where the time goes in v3:
time: 360 us; the launch traced here: 358 us
  Pallas kernels  229 us (64%)
  matrix products  49 us (14%)
  other arithmetic  40.1 us (11%)
  local copies, waits for them, and re-layouts  29.5 us (8%)
  between operations  10.3 us (3%)
    pallas_call x1, Pallas kernels, enter(): pl.pallas_call(functools.partial(enter_kernel, n), out_shape=(jax.ShapeDt...  73.9 us
    pallas_call x1, Pallas kernels, ring_sum(): pl.pallas_call(functools.partial(ring_sum_kernel, n, axis, tuple(pieces),...  71.7 us
    pallas_call x4, Pallas kernels, scatter_sum(): pl.pallas_call(functools.partial(scatter_sum_kernel, axis), out_shape=jax...  34.6 us
    pallas_call x2, Pallas kernels, ring_gather(): pl.pallas_call(functools.partial(ring_gather_kernel, n, axis), out_shape=...  32.8 us
    pallas_call x2, Pallas kernels, gather(): pl.pallas_call(functools.partial(gather_kernel, axis), out_shape=jax.Shap...  16.3 us
    unnamed x168, local copies, waits for them, and re-layouts  9.1 us
    dot_general x11, matrix products, advance(): jnp.einsum('zsb,sbi->zsi', query_decayed, memory_state, precision=HIGH_PR...  7.32 us
    dot_general x11, matrix products, advance(): jnp.einsum('zie,zir->ier', key_final_rows, value_segment, precision=HIGH_...  7.22 us

profile of v3, /device:TPU:0, one launch (start us, length us, event | category | flops | bytes accessed | tf_op | source)
XLA Modules:
  0.0 358.1 jit_solution(15204405919567190578)
XLA Ops:
  4.1 1.8 pad_maximum_fusion.2.x_ref
  12.0 73.9 %shard_map.288 = (bf16[8,128,3328]{2,1,0:T(8,128)(2,1)}, f32[4,64,2048]{2,1,0:T(8,128)}) custom-call(bf16[128,3328]{1,0:T(8,128)(2,1)} %concatenate.81.w_ref, f32[64,2048]{1,0:T(8,128)} %pad_maximum_fusion.2.x_ref), custom_call_target="tpu_custom_call" | custom-call | tf_op jit(solution)/shard_map/pallas_call | solution.py:208
  92.6 2.0 fusion.15
  99.9 16.8 %shard_map.289 = bf16[8,144,256]{2,1,0:T(8,128)(2,1)} custom-call(bf16[144,256]{1,0:T(8,128)(2,1)} %pad_maximum_fusion.9.x_ref), custom_call_target="tpu_custom_call" | custom-call | tf_op jit(solution)/shard_map/pallas_call | solution.py:114
  122.1 3.9 %compare_convert_fusion = (f32[64]{0:T(128)}, f32[64]{0:T(128)S(1)}, f32[64]{0:T(128)S(1)}, f32[64]{0:T(128)S(1)}, f32[64]{0:T(128)S(1)}, /*index=5*/f32[64]{0:T(128)S(1)}, f32[64]{0:T(128)S(1)}, f32[64]{0:T(128)S(1)}) fusion(f32[]{:T(128)} %bitcast.27, f32[256]{0:T(256)S(1)} %convert_add_fusion, f32[]{:T(128)} %fusion.227, f32[]{:T(128)} %bitcast.41, ...), kind=kLoop, calls=%fused_computation.385 | loop fusion | flops 1024 | bytes 3092 | tf_op jit(solution)/shard_map/jvp()/eval_jaxpr/convert_element_type | solution.py:428
  136.0 2.3 convolution_convert_fusion.4
  138.3 8.8 %shard_map.290 = f32[64,1024]{1,0:T(8,128)} custom-call(bf16[4,64,1024]{2,1,0:T(8,128)(2,1)} %bitcast.691), custom_call_target="tpu_custom_call" | custom-call | tf_op jit(solution)/shard_map/pallas_call | solution.py:352
  149.5 8.2 %shard_map.291 = bf16[4,64,1024]{2,1,0:T(8,128)(2,1)} custom-call(bf16[64,1024]{1,0:T(8,128)(2,1)} %multiply_convert_fusion.5.x_ref), custom_call_target="tpu_custom_call" | custom-call | tf_op jit(solution)/shard_map/pallas_call | solution.py:183
  157.8 3.1 fusion.5
  162.2 2.3 multiply_convert_fusion.2
  167.4 12.1 %shard_map.292 = f32[64,2048]{1,0:T(8,128)} custom-call(bf16[4,64,2048]{2,1,0:T(8,128)(2,1)} %bitcast.684), custom_call_target="tpu_custom_call" | custom-call | tf_op jit(solution)/shard_map/pallas_call | solution.py:352
  179.5 1.6 multiply_reduce_fusion.2
  181.2 2.0 fusion.247
  183.2 8.0 %shard_map.293 = bf16[4,64,1024]{2,1,0:T(8,128)(2,1)} custom-call(bf16[64,1024]{1,0:T(8,128)(2,1)} %get-tuple-element.184.x_ref), custom_call_target="tpu_custom_call" | custom-call | tf_op jit(solution)/shard_map/pallas_call | solution.py:183
  191.2 2.8 fusion.74
  198.4 15.9 %shard_map.294 = bf16[8,144,256]{2,1,0:T(8,128)(2,1)} custom-call(bf16[144,256]{1,0:T(8,128)(2,1)} %pad_maximum_fusion.10.x_ref), custom_call_target="tpu_custom_call" | custom-call | tf_op jit(solution)/shard_map/pallas_call | solution.py:114
  244.8 2.9 fusion.20
  247.7 8.1 %shard_map.295 = f32[64,1024]{1,0:T(8,128)} custom-call(bf16[4,64,1024]{2,1,0:T(8,128)(2,1)} %bitcast.699), custom_call_target="tpu_custom_call" | custom-call | tf_op jit(solution)/shard_map/pallas_call | solution.py:352
  255.8 1.8 multiply_reduce_fusion.3
  259.4 2.5 fusion.8.refs_3_
  262.0 2.6 convolution_convert_fusion
  265.7 1.8 convolution_convert_fusion.1
  267.6 71.7 %shard_map.296 = (f32[128,768]{1,0:T(8,128)}, f32[128,256]{1,0:T(8,128)}, f32[128,1408]{1,0:T(8,128)}, f32[128,896]{1,0:T(8,128)}) custom-call(bf16[8,128,768]{2,1,0:T(8,128)(2,1)} %bitcast.696, bf16[8,128,256]{2,1,0:T(8,128)(2,1)} %bitcast.695, bf16[8,128,1408]{2,1,0:T(8,128)(2,1)} %bitcast.625, bf16[8,128,896]{2,1,0:T(8,128)(2,1)} %fusion.8.refs_3_), custom_call_target="tpu_custom_call" | custom-call | tf_op jit(solution)/shard_map/pallas_call | solution.py:293
  344.5 5.6 %shard_map.297 = f32[64,128]{1,0:T(8,128)} custom-call(bf16[4,64,128]{2,1,0:T(8,128)(2,1)} %pad.114.x_ref), custom_call_target="tpu_custom_call" | custom-call | tf_op jit(solution)/shard_map/pallas_call | solution.py:352
  (358 shorter events, 85.2 us)
Async XLA Ops:
  0.7 10.0 %copy-start.33 = (bf16[128,128]{1,0:T(8,128)(2,1)S(1)}, bf16[128,128]{1,0:T(8,128)(2,1)}, u32[]{:S(2)}) copy-start(bf16[128,128]{1,0:T(8,128)(2,1)} %param.33) | copy-start | bytes 98308
  0.7 10.0 %copy-start.34 = (bf16[128,128]{1,0:T(8,128)(2,1)S(1)}, bf16[128,128]{1,0:T(8,128)(2,1)}, u32[]{:S(2)}) copy-start(bf16[128,128]{1,0:T(8,128)(2,1)} %param.34) | copy-start | bytes 98308
  88.0 147.8 %copy-start.1 = (bf16[4,64,1024]{2,1,0:T(8,128)(2,1)}, bf16[4,64,1024]{2,1,0:T(8,128)(2,1)S(1)}, u32[]{:S(2)}) copy-start(bf16[4,64,1024]{2,1,0:T(8,128)(2,1)S(1)} %multiply_convert_fusion) | copy-start | bytes 1572868
  129.6 17.6 %copy-start = (f32[64,1024]{1,0:T(8,128)S(1)}, f32[64,1024]{1,0:T(8,128)}, u32[]{:S(2)}) copy-start(f32[64,1024]{1,0:T(8,128)} %param.29) | copy-start | bytes 786436
  148.8 12.1 %copy-start.65 = (f32[64]{0:T(128)}, f32[64]{0:T(128)S(1)}, u32[]{:S(2)}) copy-start(f32[64]{0:T(128)S(1)} %get-tuple-element.241) | copy-start | bytes 772
  166.4 14.8 %copy-start.13 = (f32[64,1024]{1,0:T(8,128)S(1)}, f32[64,1024]{1,0:T(8,128)}, u32[]{:S(2)}) copy-start(f32[64,1024]{1,0:T(8,128)} %param.30) | copy-start | bytes 786436
  183.2 11.7 %copy-start.42 = (s32[256]{0:T(256)S(1)}, s32[256]{0:T(256)}, u32[]{:S(2)}) copy-start(s32[256]{0:T(256)} %param.31) | copy-start | bytes 3076
  194.9 31.8 %copy-start.38 = (f32[64]{0:T(128)S(1)}, f32[64]{0:T(128)}, u32[]{:S(2)}) copy-start(f32[64]{0:T(128)} %copy-done.37) | copy-start | bytes 772
  194.9 32.2 %copy-start.47 = (f32[64]{0:T(128)S(1)}, f32[64]{0:T(128)}, u32[]{:S(2)}) copy-start(f32[64]{0:T(128)} %copy-done.46) | copy-start | bytes 772
  217.8 15.4 %copy-start.36 = (f32[64]{0:T(128)S(1)}, f32[64]{0:T(128)}, u32[]{:S(2)}) copy-start(f32[64]{0:T(128)} %copy-done.35) | copy-start | bytes 772
  219.1 14.4 %copy-start.49 = (f32[64]{0:T(128)S(1)}, f32[64]{0:T(128)}, u32[]{:S(2)}) copy-start(f32[64]{0:T(128)} %copy-done.48) | copy-start | bytes 772
  220.2 13.8 %copy-start.56 = (f32[128]{0:T(128)S(1)}, f32[128]{0:T(128)}, u32[]{:S(2)}) copy-start(f32[128]{0:T(128)} %copy-done.55) | copy-start | bytes 1540
  222.4 13.1 %copy-start.21 = (f32[256,128]{1,0:T(8,128)S(1)}, f32[256,128]{1,0:T(8,128)}, u32[]{:S(2)}) copy-start(f32[256,128]{1,0:T(8,128)} %get-tuple-element.243) | copy-start | bytes 393220
  244.7 11.1 %copy-start.64 = (f32[64]{0:T(128)S(1)}, f32[64]{0:T(128)}, u32[]{:S(2)}) copy-start(f32[64]{0:T(128)} %copy-done.63) | copy-start | bytes 772
  244.7 12.9 %copy-start.73 = (bf16[256]{0:T(256)(128)(2,1)S(1)}, bf16[256]{0:T(256)(128)(2,1)}, u32[]{:S(2)}) copy-start(bf16[256]{0:T(256)(128)(2,1)} %get-tuple-element.164) | copy-start | bytes 1540
  244.7 13.0 %copy-start.52 = (bf16[1024]{0:T(1024)(128)(2,1)S(1)}, bf16[1024]{0:T(1024)(128)(2,1)}, u32[]{:S(2)}) copy-start(bf16[1024]{0:T(1024)(128)(2,1)} %get-tuple-element.166) | copy-start | bytes 6148
  244.7 13.0 %copy-start.7 = (bf16[4,64,1024]{2,1,0:T(8,128)(2,1)S(1)}, bf16[4,64,1024]{2,1,0:T(8,128)(2,1)}, u32[]{:S(2)}) copy-start(bf16[4,64,1024]{2,1,0:T(8,128)(2,1)} %copy-done.6) | copy-start | bytes 1572868
  244.8 13.0 %copy-start.19 = (bf16[256,704]{1,0:T(8,128)(2,1)S(1)}, bf16[256,704]{1,0:T(8,128)(2,1)}, u32[]{:S(2)}) copy-start(bf16[256,704]{1,0:T(8,128)(2,1)} %copy-done.18) | copy-start | bytes 1081348
  339.3 14.7 %copy-start.20 = (f32[128,768]{1,0:T(8,128)S(1)}, f32[128,768]{1,0:T(8,128)}, u32[]{:S(2)}) copy-start(f32[128,768]{1,0:T(8,128)} %get-tuple-element.97) | copy-start | bytes 1179652
  339.3 16.0 %copy-start.22 = (f32[128,256]{1,0:T(8,128)S(1)}, f32[128,256]{1,0:T(8,128)}, u32[]{:S(2)}) copy-start(f32[128,256]{1,0:T(8,128)} %get-tuple-element.98) | copy-start | bytes 393220
  340.7 16.6 %copy-start.74 = (f32[64]{0:T(128)S(1)}, f32[64]{0:T(128)}, u32[]{:S(2)}) copy-start(f32[64]{0:T(128)} %get-tuple-element.171) | copy-start | bytes 772
  340.7 16.6 %copy-start.4 = (f32[64,1024]{1,0:T(8,128)S(1)}, f32[64,1024]{1,0:T(8,128)}, u32[]{:S(2)}) copy-start(f32[64,1024]{1,0:T(8,128)} %shard_map.295) | copy-start | bytes 786436
  340.7 16.6 %copy-start.12 = (f32[64,1024]{1,0:T(8,128)S(1)}, f32[64,1024]{1,0:T(8,128)}, u32[]{:S(2)}) copy-start(f32[64,1024]{1,0:T(8,128)} %get-tuple-element.185) | copy-start | bytes 786436
  340.7 16.6 %copy-start.72 = (f32[64]{0:T(128)S(1)}, f32[64]{0:T(128)}, u32[]{:S(2)}) copy-start(f32[64]{0:T(128)} %get-tuple-element.238) | copy-start | bytes 772
  (55 other events, 296.6 us)
